TPU v7x, 512 devices: a whole 4x4x16 slice. The times are simulated.
512 devices in a mesh: ta: 32 (over y, x, core), sa: 16 (over z).
Axes of the slice: x: 4, y: 4, z: 16, core: 2. Of those that a mesh axis runs over, the one named last changes fastest.
Arguments:
- eigenvectors: bfloat16 [32, 256, 2, 3, 16, 384], P('ta', None, None, None, 'sa'), may hold values from -17 to 17
- momenta: int32 [8, 3], replicated, may hold values from -4 to 4
- block_order: int32 [4], replicated, may hold values from 0 to 3, each once
Outputs:
- meson_fields: float32 [8, 16, 64, 32, 128], P(None, 'sa', 'ta')
- slice_norms: float32 [32, 256], P('ta')
Inputs may be any that keep to these rules, and one draw needn't show every extreme that they name: block_order names every block once.
All inputs are finite; a program needn't handle non-finite values.
Results may differ from a plain program's by a relative error of at most 0.0018.
Values sent between devices are 32-bit elements; how exact they have to be, the bound alone decides.
No kernel may reach another device: no remote copies, remote signals or barrier semaphores. Data moves between devices by JAX's collectives and lax.ppermute only.
A program may use at most 64 MiB of HBM per device.

v0:
```python
import math

import jax
import jax.numpy as jnp
from jax import lax
from jax.sharding import Mesh
from jax.sharding import PartitionSpec as P

NC = 3
BS = 64
NBLK = 4
LX = 96
TA = ("ta_0", "ta_1", "ta_2")


full_turn = 2.0 * math.pi


def from_everyone(array, axis):
    copies = jnp.broadcast_to(array, (lax.axis_size(axis), *array.shape))
    return lax.all_to_all(copies, axis, split_axis=0, concat_axis=0, tiled=True)


def taken_together(array, axis):
    everything = from_everyone(array, axis)
    return jnp.sum(everything, axis=0)


def cut_along(array, dim, peers):
    before, after = (array.shape[:dim], array.shape[dim + 1 :])
    return jnp.moveaxis(array.reshape(*before, peers, -1, *after), dim, 0)


def laid_out(tiles, dim):
    tiles = jnp.moveaxis(tiles, 0, dim)
    dims = tiles.shape
    return tiles.reshape(*dims[:dim], dims[dim] * dims[dim + 1], *dims[dim + 2 :])


def turned_blocks(tiles, axes, sequence):
    inside = tiles.shape[1:]
    filled = tiles.reshape(*(lax.axis_size(a) for a in axes), *inside)
    for k in sequence:
        filled = lax.all_to_all(filled, axes[k], k, k, tiled=True)
    return filled.reshape(-1, *inside)


def two_step_exchange(array, groups, sequence, split_dim, concat_dim):
    peers = lax.axis_size(groups[0]) * lax.axis_size(groups[1])
    tiles = cut_along(array, split_dim, peers)
    return laid_out(turned_blocks(tiles, groups, sequence), concat_dim)


def phased_right(blocks, cos_table, sin_table):
    real_part = blocks[:, :, 0].astype(jnp.float32)[None]
    imag_part = blocks[:, :, 1].astype(jnp.float32)[None]
    cos_full = cos_table[:, None, None, None, :]
    sin_full = sin_table[:, None, None, None, :]
    phased_re = (real_part * cos_full + imag_part * sin_full).astype(jnp.bfloat16)
    phased_im = (imag_part * cos_full - real_part * sin_full).astype(jnp.bfloat16)
    first_half = jnp.stack([phased_re, phased_im], axis=3)
    second_half = jnp.stack([phased_im, -phased_re], axis=3)
    right_cols = jnp.stack([first_half, second_half], axis=1)
    return right_cols.reshape(right_cols.shape[0], 2, right_cols.shape[2], right_cols.shape[3], -1)


def spatial_norms(slab_data, plane_count, planes):
    local_sums = jnp.sum(jnp.square(slab_data.astype(jnp.float32)), axis=(2, 3, 4)).reshape(-1)
    summed = taken_together(local_sums, "sa")
    return (summed / (2 * NC * plane_count * planes))[None, :]


def body(eigenvectors, momenta, block_order):
    planes = eigenvectors.shape[-1]
    plane_count = lax.axis_size("sa")
    slab_data = eigenvectors.reshape(NBLK, BS, 2, NC, planes)
    ordered = jnp.take(slab_data, block_order, axis=0)
    left_rows = ordered.reshape(NBLK, BS, 2 * NC * planes)
    site_index = jnp.arange(planes, dtype=jnp.int32)
    x_coord = site_index % LX
    y_coord = site_index // LX
    z_coord = lax.axis_index("sa")
    phase_index = (
        momenta[:, 0:1] * x_coord[None, :]
        + momenta[:, 1:2] * y_coord[None, :]
        + momenta[:, 2:3] * z_coord
    )
    phase_index = jnp.mod(phase_index, LX)
    angles = phase_index.astype(jnp.float32) * (full_turn / LX)
    cosines = jnp.cos(angles)
    sine_vals = jnp.sin(angles)
    norm_scale = 1.0 / math.sqrt(2 * NC * plane_count * planes)

    def one_momentum(trig_pair):
        right_cols = phased_right(ordered, trig_pair[0], trig_pair[1])[0]
        product = jnp.einsum(
            "ark,cbjk->abrcj", left_rows, right_cols, preferred_element_type=jnp.float32
        )
        return product.reshape(NBLK * NBLK, BS, 2 * BS)

    fields = lax.map(one_momentum, (cosines[:, None, :], sine_vals[:, None, :]))
    owned_sums = lax.psum_scatter(fields, "sa", scatter_dimension=1, tiled=True)
    expanded = (owned_sums * norm_scale)[:, :, :, None, :]
    meson_fields = two_step_exchange(expanded, (("ta_0", "ta_1"), "ta_2"), (1, 0), 2, 3)
    slice_norms = spatial_norms(slab_data, plane_count, planes)
    return (meson_fields, slice_norms)


def solution(mesh):
    finer = Mesh(mesh.devices.reshape(4, 4, 2, mesh.shape["sa"]), ("ta_0", "ta_1", "ta_2", "sa"))
    placed = (P(TA, None, None, None, "sa", None), P(), P())
    return jax.shard_map(
        body,
        mesh=finer,
        in_specs=placed,
        out_specs=(P(None, "sa", TA, None, None), P(TA, None)),
        check_vma=False,
    )
```

profile of v0, /device:TPU:1, one launch (start us, length us, event | category | flops | bytes accessed | tf_op | source)
XLA Modules:
  0.0 400.9 jit_solution(12368125932572685747)
XLA Ops:
  11.9 2.2 gather.7
  17.8 174.8 %while.10 = (s32[]{:T(128)}, f32[8,16,64,128]{3,2,1,0:T(8,128)}, bf16[4,64,2,3,384]{4,3,1,0,2:T(4,128)(2,1)S(1)}, f32[8,1,384]{2,0,1:T(8,128)S(1)}, f32[8,1,384]...) while((s32[]{:T(128)}, f32[8,16,64,128]{3,2,1,0:T(8,128)}, ...), condition=%wide.region_1.2_spmd, body=%wide.region_0.1_spmd.sunk | while | flops 613711872 | bytes 29635180 | solution.py:101
  19.3 1.8 pad_maximum_fusion.3
  21.1 1.7 copy.95
  22.8 4.0 stack.21
  28.5 4.1 %stack.22 = bf16[1,4,64,2304]{3,2,1,0:T(8,128)(2,1)} reshape(bf16[1,4,64,2,3,384]{5,4,3,2,1,0:T(4,128)(2,1)} %copy.96) | data formatting | bytes 2359296 | tf_op jit(solution)/shard_map/while/body/eval_jaxpr/stack | solution.py:63
  32.6 4.0 fusion.31
  41.1 1.8 pad_maximum_fusion.3
  42.9 1.7 copy.95
  44.7 4.0 stack.21
  50.4 4.1 %stack.22 = bf16[1,4,64,2304]{3,2,1,0:T(8,128)(2,1)} reshape(bf16[1,4,64,2,3,384]{5,4,3,2,1,0:T(4,128)(2,1)} %copy.96) | data formatting | bytes 2359296 | tf_op jit(solution)/shard_map/while/body/eval_jaxpr/stack | solution.py:63
  54.5 4.0 fusion.31
  63.0 1.8 pad_maximum_fusion.3
  64.8 1.7 copy.95
  66.5 4.0 stack.21
  72.2 4.1 %stack.22 = bf16[1,4,64,2304]{3,2,1,0:T(8,128)(2,1)} reshape(bf16[1,4,64,2,3,384]{5,4,3,2,1,0:T(4,128)(2,1)} %copy.96) | data formatting | bytes 2359296 | tf_op jit(solution)/shard_map/while/body/eval_jaxpr/stack | solution.py:63
  76.3 4.0 fusion.31
  84.8 1.8 pad_maximum_fusion.3
  86.6 1.7 copy.95
  88.4 4.0 stack.21
  94.1 4.1 %stack.22 = bf16[1,4,64,2304]{3,2,1,0:T(8,128)(2,1)} reshape(bf16[1,4,64,2,3,384]{5,4,3,2,1,0:T(4,128)(2,1)} %copy.96) | data formatting | bytes 2359296 | tf_op jit(solution)/shard_map/while/body/eval_jaxpr/stack | solution.py:63
  98.2 4.0 fusion.31
  106.7 1.8 pad_maximum_fusion.3
  108.5 1.7 copy.95
  110.2 4.0 stack.21
  115.9 4.1 %stack.22 = bf16[1,4,64,2304]{3,2,1,0:T(8,128)(2,1)} reshape(bf16[1,4,64,2,3,384]{5,4,3,2,1,0:T(4,128)(2,1)} %copy.96) | data formatting | bytes 2359296 | tf_op jit(solution)/shard_map/while/body/eval_jaxpr/stack | solution.py:63
  120.0 4.0 fusion.31
  128.5 1.8 pad_maximum_fusion.3
  130.3 1.7 copy.95
  132.1 4.0 stack.21
  137.8 4.1 %stack.22 = bf16[1,4,64,2304]{3,2,1,0:T(8,128)(2,1)} reshape(bf16[1,4,64,2,3,384]{5,4,3,2,1,0:T(4,128)(2,1)} %copy.96) | data formatting | bytes 2359296 | tf_op jit(solution)/shard_map/while/body/eval_jaxpr/stack | solution.py:63
  141.9 4.0 fusion.31
  150.4 1.8 pad_maximum_fusion.3
  152.2 1.7 copy.95
  153.9 4.0 stack.21
  159.6 4.1 %stack.22 = bf16[1,4,64,2304]{3,2,1,0:T(8,128)(2,1)} reshape(bf16[1,4,64,2,3,384]{5,4,3,2,1,0:T(4,128)(2,1)} %copy.96) | data formatting | bytes 2359296 | tf_op jit(solution)/shard_map/while/body/eval_jaxpr/stack | solution.py:63
  163.8 4.0 fusion.31
  172.2 1.8 pad_maximum_fusion.3
  175.8 4.0 stack.21
  181.5 4.1 %stack.22 = bf16[1,4,64,2304]{3,2,1,0:T(8,128)(2,1)} reshape(bf16[1,4,64,2,3,384]{5,4,3,2,1,0:T(4,128)(2,1)} %copy.96) | data formatting | bytes 2359296 | tf_op jit(solution)/shard_map/while/body/eval_jaxpr/stack | solution.py:63
  185.6 4.0 fusion.31
  194.0 1.8 multiply_reduce_fusion
  195.8 149.9 %all-reduce.3.cloned.1.call-done = f32[8,16,64,128]{3,2,1,0:T(8,128)} async-done(((f32[8,16,64,128]{3,2,1,0:T(8,128)}), f32[8,16,64,128]{3,2,1,0:T(8,128)}) %all-reduce.3.cloned.1.call-update) | async-done | bytes 4194320
  347.7 13.0 %all_to_all.16 = f32[16,2,8,1,2,1,128]{6,0,4,2,5,3,1:T(8,128)S(1)} all-to-all(f32[16,2,8,1,2,1,128]{6,0,4,2,5,3,1:T(8,128)S(1)} %copy.78), channel_id=1, replica_groups=mesh['ta_0'=4,'ta_1'=4,'ta_2'=2,'sa'=16] {'ta_2'}, dimensions={1} | all-to-all | bytes 524288 | tf_op jit(solution)/shard_map/all_to_all | solution.py:44
  361.3 6.5 %all-to-all-start.2 = ((f32[16,1,256]{2,1,0:T(1,128)}), f32[16,1,256]{2,1,0:T(1,128)S(1)}, u32[]{:S(2)}, u32[]{:S(2)}) async-start(f32[16,1,256]{2,1,0:T(1,128)} %broadcast_in_dim.41), calls=%async_computation.2 | async-start | bytes 32768 | tf_op jit(solution)/shard_map/all_to_all | solution.py:21
  368.7 10.5 %all-to-all-done.2 = f32[16,1,256]{2,1,0:T(1,128)S(1)} async-done(((f32[16,1,256]{2,1,0:T(1,128)}), f32[16,1,256]{2,1,0:T(1,128)S(1)}, u32[]{:S(2)}, u32[]{:S(2)}) %all-to-all-start.2) | async-done | bytes 16416 | tf_op jit(solution)/shard_map/all_to_all | solution.py:21
  379.2 6.5 %all-to-all-start.1 = ((f32[16,2,8,1,2,1,128]{6,1,4,2,5,3,0:T(2,128)}), f32[16,2,8,1,2,1,128]{6,1,4,2,5,3,0:T(2,128)S(1)}, u32[]{:S(2)}, u32[]{:S(2)}) async-start(f32[16,2,8,1,2,1,128]{6,1,4,2,5,3,0:T(2,128)} %copy.79), calls=%async_computation.1 | async-start | bytes 524288 | tf_op jit(solution)/shard_map/all_to_all | solution.py:44
  386.3 6.9 %all-to-all-done.1 = f32[16,2,8,1,2,1,128]{6,1,4,2,5,3,0:T(2,128)S(1)} async-done(((f32[16,2,8,1,2,1,128]{6,1,4,2,5,3,0:T(2,128)}), f32[16,2,8,1,2,1,128]{6,1,4,2,5,3,0:T(2,128)S(1)}, u32[]{:S(2)}, u32[]{:S(2)}) %all-to-all-start.1) | async-done | bytes 262176 | tf_op jit(solution)/shard_map/all_to_all | solution.py:44
  (104 shorter events, 65.8 us)
Async XLA Ops:
  7.2 338.5 %all-reduce.3.cloned.1.call-start = ((), (), s32[]{:S(2)}) async-start(), calls=%async_computation.3 | async-start | bytes 8388608
  14.1 1.3 copy-start.2
  16.6 1.0 copy-start.3
  28.5 4.1 %copy-start = (bf16[1,4,64,2304]{3,2,1,0:T(8,128)(2,1)S(1)}, bf16[1,4,64,2304]{3,2,1,0:T(8,128)(2,1)}, u32[]{:S(2)}) copy-start(bf16[1,4,64,2304]{3,2,1,0:T(8,128)(2,1)} %stack.21) | copy-start | bytes 3538948 | tf_op jit(solution)/shard_map/while
  50.4 4.1 %copy-start = (bf16[1,4,64,2304]{3,2,1,0:T(8,128)(2,1)S(1)}, bf16[1,4,64,2304]{3,2,1,0:T(8,128)(2,1)}, u32[]{:S(2)}) copy-start(bf16[1,4,64,2304]{3,2,1,0:T(8,128)(2,1)} %stack.21) | copy-start | bytes 3538948 | tf_op jit(solution)/shard_map/while
  72.2 4.1 %copy-start = (bf16[1,4,64,2304]{3,2,1,0:T(8,128)(2,1)S(1)}, bf16[1,4,64,2304]{3,2,1,0:T(8,128)(2,1)}, u32[]{:S(2)}) copy-start(bf16[1,4,64,2304]{3,2,1,0:T(8,128)(2,1)} %stack.21) | copy-start | bytes 3538948 | tf_op jit(solution)/shard_map/while
  94.1 4.1 %copy-start = (bf16[1,4,64,2304]{3,2,1,0:T(8,128)(2,1)S(1)}, bf16[1,4,64,2304]{3,2,1,0:T(8,128)(2,1)}, u32[]{:S(2)}) copy-start(bf16[1,4,64,2304]{3,2,1,0:T(8,128)(2,1)} %stack.21) | copy-start | bytes 3538948 | tf_op jit(solution)/shard_map/while
  115.9 4.1 %copy-start = (bf16[1,4,64,2304]{3,2,1,0:T(8,128)(2,1)S(1)}, bf16[1,4,64,2304]{3,2,1,0:T(8,128)(2,1)}, u32[]{:S(2)}) copy-start(bf16[1,4,64,2304]{3,2,1,0:T(8,128)(2,1)} %stack.21) | copy-start | bytes 3538948 | tf_op jit(solution)/shard_map/while
  137.8 4.1 %copy-start = (bf16[1,4,64,2304]{3,2,1,0:T(8,128)(2,1)S(1)}, bf16[1,4,64,2304]{3,2,1,0:T(8,128)(2,1)}, u32[]{:S(2)}) copy-start(bf16[1,4,64,2304]{3,2,1,0:T(8,128)(2,1)} %stack.21) | copy-start | bytes 3538948 | tf_op jit(solution)/shard_map/while
  159.6 4.1 %copy-start = (bf16[1,4,64,2304]{3,2,1,0:T(8,128)(2,1)S(1)}, bf16[1,4,64,2304]{3,2,1,0:T(8,128)(2,1)}, u32[]{:S(2)}) copy-start(bf16[1,4,64,2304]{3,2,1,0:T(8,128)(2,1)} %stack.21) | copy-start | bytes 3538948 | tf_op jit(solution)/shard_map/while
  181.5 4.1 %copy-start = (bf16[1,4,64,2304]{3,2,1,0:T(8,128)(2,1)S(1)}, bf16[1,4,64,2304]{3,2,1,0:T(8,128)(2,1)}, u32[]{:S(2)}) copy-start(bf16[1,4,64,2304]{3,2,1,0:T(8,128)(2,1)} %stack.21) | copy-start | bytes 3538948 | tf_op jit(solution)/shard_map/while
  192.6 1.4 copy-start.1
  361.3 17.9 %all-to-all-start.2 = ((f32[16,1,256]{2,1,0:T(1,128)}), f32[16,1,256]{2,1,0:T(1,128)S(1)}, u32[]{:S(2)}, u32[]{:S(2)}) async-start(f32[16,1,256]{2,1,0:T(1,128)} %broadcast_in_dim.41), calls=%async_computation.2 | async-start | bytes 32768 | tf_op jit(solution)/shard_map/all_to_all | solution.py:21
  379.2 14.1 %all-to-all-start.1 = ((f32[16,2,8,1,2,1,128]{6,1,4,2,5,3,0:T(2,128)}), f32[16,2,8,1,2,1,128]{6,1,4,2,5,3,0:T(2,128)S(1)}, u32[]{:S(2)}, u32[]{:S(2)}) async-start(f32[16,2,8,1,2,1,128]{6,1,4,2,5,3,0:T(2,128)} %copy.79), calls=%async_computation.1 | async-start | bytes 524288 | tf_op jit(solution)/shard_map/all_to_all | solution.py:44
Sparse Core Ops, SparseCore 0:
  192.8 152.8 all-reduce.2
where the time goes:
time: 404 us; the launch traced here: 401 us
  waiting for transfers between devices  167 us (41%)
  local copies, waits for them, and re-layouts  128 us (32%)
  other arithmetic  32.8 us (8%)
  matrix products  32 us (8%)
  between operations  14.1 us (3%)
  starting transfers between devices  13 us (3%)
  blocking collectives  13 us (3%)
    unnamed x2, waiting for transfers between devices  150 us
    another operation x16, local copies, waits for them, and re-layouts, phased_right(): right_cols = jnp.stack([first_half, second_half], axis=1)  64.7 us
    dot_general x8, matrix products, one_momentum(): jnp.einsum('ark,cbjk->abrcj', left_rows, right_cols, preferred_element_ty...  32 us
    another operation x8, other arithmetic, phased_right(): first_half = jnp.stack([phased_re, phased_im], axis=3)  14.5 us
    another operation x8, local copies, waits for them, and re-layouts, phased_right(): second_half = jnp.stack([phased_im, -phased_re], axis=3)  13.9 us
    another operation x8, local copies, waits for them, and re-layouts, phased_right(): first_half = jnp.stack([phased_re, phased_im], axis=3)  13.8 us
    all_to_all x1, blocking collectives, turned_blocks(): filled = lax.all_to_all(filled, axes[k], k, k, tiled=True)  13 us
    transpose x8, local copies, waits for them, and re-layouts, one_momentum(): jnp.einsum('ark,cbjk->abrcj', left_rows, right_cols, preferred_element_ty...  12.7 us
  transfers between devices with their start and end apart: 3, of which 3 were waited for; matrix products, arithmetic and copies ran while one was open for 1% of the time, Pallas kernels for 0%

commit v1 on v0

v1 whole, which is shorter than its diff:
```python
import math

import jax
import jax.numpy as jnp
from jax import lax
from jax.experimental import pallas as pl
from jax.experimental.pallas import tpu as pltpu
from jax.sharding import PartitionSpec as P

NC = 3
BS = 64
NBLK = 4
NV = NBLK * BS
LX = 96
PARTS = 2 * NC
full_turn = 2.0 * math.pi


def fields_kernel(planes, scale, order_ref, mom_ref, x_ref, out_ref, nrm_ref, left_ref, right_ref, cos_ref, sin_ref):
    p = pl.program_id(0)
    half = NC * planes

    @pl.when(p == 0)
    def _():
        site = lax.broadcasted_iota(jnp.int32, (mom_ref.shape[0], planes), 1).astype(jnp.float32)
        y = jnp.floor((site + 0.5) * (1.0 / LX))
        x = site - LX * y
        z = lax.axis_index("sa").astype(jnp.float32)
        mom = mom_ref[...].astype(jnp.float32)
        index = mom[:, 0:1] * x + mom[:, 1:2] * y + mom[:, 2:3] * z
        index = index - LX * jnp.floor((index + 0.5) * (1.0 / LX))
        angles = index * (full_turn / LX)
        cos_ref[...] = jnp.cos(angles)
        sin_ref[...] = jnp.sin(angles)
        for a in range(NBLK):
            rows = pl.ds(pl.multiple_of(order_ref[a] * BS, BS), BS)
            for c in range(NC):
                re = x_ref[c, rows, :]
                im = x_ref[NC + c, rows, :]
                lanes, after = pl.ds(c * planes, planes), pl.ds(half + c * planes, planes)
                left_ref[pl.ds(a * BS, BS), lanes] = re
                left_ref[pl.ds(a * BS, BS), after] = im
                left_ref[pl.ds(NV + a * BS, BS), lanes] = -im
                left_ref[pl.ds(NV + a * BS, BS), after] = re
        squares = jnp.zeros((NV, 128), jnp.float32)
        for k in range(PARTS):
            for l in range(planes // 128):
                v = x_ref[k, :, pl.ds(l * 128, 128)].astype(jnp.float32)
                squares = squares + v * v
        nrm_ref[...] = jnp.sum(squares.T, axis=0, keepdims=True)

    cos = cos_ref[pl.ds(p, 1), :]
    sin = sin_ref[pl.ds(p, 1), :]
    for c in range(NC):
        lanes, after = pl.ds(c * planes, planes), pl.ds(half + c * planes, planes)
        re = left_ref[pl.ds(0, NV), lanes].astype(jnp.float32)
        im = left_ref[pl.ds(0, NV), after].astype(jnp.float32)
        right_ref[:, lanes] = (re * cos + im * sin).astype(jnp.bfloat16)
        right_ref[:, after] = (im * cos - re * sin).astype(jnp.bfloat16)
    product = lax.dot_general(
        left_ref[...], right_ref[...], (((1,), (1,)), ((), ())), preferred_element_type=jnp.float32
    )
    product = product * scale
    low = lax.broadcasted_iota(jnp.int32, (NV, 128), 1) < BS
    for tile in range(NV // 128):
        real = product[:NV, tile * 128 : (tile + 1) * 128]
        imag = product[NV:, tile * 128 : (tile + 1) * 128]
        first = jnp.where(low, real, pltpu.roll(imag, BS, 1))
        second = jnp.where(low, pltpu.roll(real, BS, 1), imag)
        for a in range(NBLK):
            out_ref[a * NBLK + 2 * tile, 0] = first[a * BS : (a + 1) * BS]
            out_ref[a * NBLK + 2 * tile + 1, 0] = second[a * BS : (a + 1) * BS]


def partial_fields(parts, momenta, block_order, scale):
    planes = parts.shape[-1]
    momenta_count = momenta.shape[0]
    pairs = NBLK * NBLK
    return pl.pallas_call(
        lambda *refs: fields_kernel(planes, scale, *refs),
        grid=(momenta_count,),
        in_specs=[
            pl.BlockSpec(memory_space=pltpu.SMEM),
            pl.BlockSpec(memory_space=pltpu.VMEM),
            pl.BlockSpec(memory_space=pltpu.VMEM),
        ],
        out_specs=[
            pl.BlockSpec((pairs, 1, BS, 2 * BS), lambda p: (0, p, 0, 0)),
            pl.BlockSpec((1, NV), lambda p: (0, 0)),
        ],
        out_shape=[
            jax.ShapeDtypeStruct((pairs, momenta_count, BS, 2 * BS), jnp.float32),
            jax.ShapeDtypeStruct((1, NV), jnp.float32),
        ],
        scratch_shapes=[
            pltpu.VMEM((2 * NV, PARTS * planes), jnp.bfloat16),
            pltpu.VMEM((NV, PARTS * planes), jnp.bfloat16),
            pltpu.VMEM((momenta_count, planes), jnp.float32),
            pltpu.VMEM((momenta_count, planes), jnp.float32),
        ],
        compiler_params=pltpu.CompilerParams(vmem_limit_bytes=40 * 1024 * 1024),
        name="fields",
    )(block_order, momenta, parts)


def body(eigenvectors, momenta, block_order):
    planes = eigenvectors.shape[-1]
    entries = 2 * NC * lax.axis_size("sa") * planes
    parts = jnp.moveaxis(eigenvectors.reshape(NV, PARTS, planes), 1, 0)
    fields, local_sums = partial_fields(parts, momenta, block_order, 1.0 / math.sqrt(entries))
    count = momenta.shape[0]
    owned = lax.psum_scatter(
        fields.reshape(NBLK * NBLK, count * BS, 2 * BS), "sa", scatter_dimension=0, tiled=True
    )
    slice_norms = lax.psum(local_sums, "sa") / entries
    peers = lax.axis_size("ta")
    tiles = jnp.moveaxis(owned.reshape(count, peers, BS // peers, 2 * BS), 1, 0)
    tiles = lax.all_to_all(tiles, "ta", 0, 0, tiled=True)
    meson_fields = jnp.transpose(tiles, (1, 2, 0, 3))[:, None]
    return (meson_fields, slice_norms)


def solution(mesh):
    return jax.shard_map(
        body,
        mesh=mesh,
        in_specs=(P("ta", None, None, None, "sa", None), P(), P()),
        out_specs=(P(None, "sa", "ta", None, None), P("ta", None)),
        check_vma=False,
    )
```

time: 404 us -> 151 us (0.37)
  the two profiles are of different devices: /device:TPU:1 before, /device:TPU:2 now
where the time goes in v1:
time: 151 us
  waiting for transfers between devices  84.5 us (56%)
  blocking collectives  28.7 us (19%)
  between operations  14.1 us (9%)
  Pallas kernels  9.35 us (6%)
  starting transfers between devices  7.27 us (5%)
  local copies, waits for them, and re-layouts  6.65 us (4%)
    reduce_scatter x1, waiting for transfers between devices, body(): lax.psum_scatter(fields.reshape(NBLK * NBLK, count * BS, 2 * BS), 'sa', s...  84.5 us
    psum x1, blocking collectives, body(): slice_norms = lax.psum(local_sums, 'sa') / entries  28.7 us
    pallas_call x1, Pallas kernels, partial_fields(): pl.pallas_call(lambda *refs: fields_kernel(planes, scale, *refs), grid=(m...  9.35 us
    all_to_all x1, starting transfers between devices, body(): tiles = lax.all_to_all(tiles, 'ta', 0, 0, tiled=True)  7.23 us
    unnamed x7, local copies, waits for them, and re-layouts  4.91 us
  transfers between devices with their start and end apart: 2, of which 1 were waited for; matrix products, arithmetic and copies ran while one was open for 0% of the time, Pallas kernels for 0%

profile of v1, /device:TPU:2, one launch (start us, length us, event | category | flops | bytes accessed | tf_op | source)
XLA Modules:
  0.0 151.1 jit_solution(6276773171148693237)
XLA Ops:
  7.2 0.0 reduce-scatter.2.cloned.1.call-start
  7.2 0.8 copy.11.refs_1_
  8.0 0.0 copy-start.1
  8.0 1.4 copy.10
  9.4 0.0 copy-done.1
  9.4 9.4 %fields.1 = (f32[16,8,64,128]{3,2,1,0:T(8,128)S(1)}, f32[1,256]{1,0:T(1,128)S(1)}) custom-call(s32[4]{0:T(128)S(1)} %copy-done.1, s32[8,3]{1,0:T(8,128)S(1)} %copy.11.refs_1_, bf16[6,256,384]{2,1,0:T(8,128)(2,1)S(1)} %bitcast.10), custom_call_target="tpu_custom_call" | custom-call | tf_op jit(solution)/shard_map/fields/pallas_call | solution.py:79
  18.8 0.0 copy-start
  18.8 1.9 %copy-done = f32[16,8,64,128]{3,2,1,0:T(8,128)} copy-done((f32[16,8,64,128]{3,2,1,0:T(8,128)}, f32[16,8,64,128]{3,2,1,0:T(8,128)S(1)}, u32[]{:S(2)}) %copy-start) | copy-done | bytes 4194328
  20.7 0.0 reduce-scatter.2.cloned.1.call-update
  20.7 84.5 %reduce-scatter.2.cloned.1.call-done = f32[1,512,128]{2,1,0:T(8,128)} async-done(((f32[16,512,128]{2,1,0:T(8,128)}), f32[1,512,128]{2,1,0:T(8,128)}) %reduce-scatter.2.cloned.1.call-update) | async-done | bytes 262160 | tf_op jit(solution)/shard_map/reduce_scatter | solution.py:112
  105.2 1.7 %copy.12 = f32[32,8,2,128]{3,2,1,0:T(2,128)} copy(f32[32,8,2,128]{3,2,0,1:T(2,128)} %bitcast.13) | data formatting | bytes 524288 | tf_op jit(solution)/shard_map/transpose | solution.py:117
  107.0 7.2 %all-to-all-start = ((f32[32,8,2,128]{3,2,1,0:T(2,128)}), f32[32,8,2,128]{3,2,1,0:T(2,128)S(1)}, u32[]{:S(2)}, u32[]{:S(2)}) async-start(f32[32,8,2,128]{3,2,1,0:T(2,128)} %copy.12), calls=%async_computation.1 | async-start | bytes 524288 | tf_op jit(solution)/shard_map/all_to_all | solution.py:118
  114.2 28.7 %psum.7 = f32[1,256]{1,0:T(1,128)S(1)} all-reduce(f32[1,256]{1,0:T(1,128)S(1)} %get-tuple-element.5), channel_id=1, replica_groups=mesh['ta'=32,'sa'=16] {'sa'}, use_global_device_ids=true, to_apply=%region_1.0 | all-reduce | flops 256 | bytes 2048 | tf_op jit(solution)/shard_map/psum | solution.py:115
  142.9 0.6 broadcast_multiply_fusion
  143.5 0.0 all-to-all-done
  143.5 0.8 copy.13
Async XLA Ops:
  7.2 98.1 %reduce-scatter.2.cloned.1.call-start = ((), (), s32[]{:S(2)}) async-start(), calls=%async_computation.2 | async-start | bytes 4456448 | tf_op jit(solution)/shard_map/reduce_scatter | solution.py:112
  8.0 1.4 copy-start.1
  18.8 1.9 %copy-start = (f32[16,8,64,128]{3,2,1,0:T(8,128)}, f32[16,8,64,128]{3,2,1,0:T(8,128)S(1)}, u32[]{:S(2)}) copy-start(f32[16,8,64,128]{3,2,1,0:T(8,128)S(1)} %get-tuple-element.4) | copy-start | bytes 12582916
  107.0 36.5 %all-to-all-start = ((f32[32,8,2,128]{3,2,1,0:T(2,128)}), f32[32,8,2,128]{3,2,1,0:T(2,128)S(1)}, u32[]{:S(2)}, u32[]{:S(2)}) async-start(f32[32,8,2,128]{3,2,1,0:T(2,128)} %copy.12), calls=%async_computation.1 | async-start | bytes 524288 | tf_op jit(solution)/shard_map/all_to_all | solution.py:118
Sparse Core Ops, SparseCore 0:
  20.9 84.3 reduce-scatter.1

commit v2 on v1

--- a/solution.py
+++ b/solution.py
@@ -112,12 +112,13 @@
     owned = lax.psum_scatter(
         fields.reshape(NBLK * NBLK, count * BS, 2 * BS), "sa", scatter_dimension=0, tiled=True
     )
-    slice_norms = lax.psum(local_sums, "sa") / entries
+    summed = lax.psum(local_sums, "sa")
+    owned, summed = lax.optimization_barrier((owned, summed))
     peers = lax.axis_size("ta")
     tiles = jnp.moveaxis(owned.reshape(count, peers, BS // peers, 2 * BS), 1, 0)
     tiles = lax.all_to_all(tiles, "ta", 0, 0, tiled=True)
     meson_fields = jnp.transpose(tiles, (1, 2, 0, 3))[:, None]
-    return (meson_fields, slice_norms)
+    return (meson_fields, summed / entries)
 
 
 def solution(mesh):

time: 151 us -> 132 us (0.87)
  the two profiles are of different devices: /device:TPU:2 before, /device:TPU:1 now
where the time goes in v2:
time: 132 us
  waiting for transfers between devices  52.9 us (40%)
  blocking collectives  30.3 us (23%)
  starting transfers between devices  17.9 us (14%)
  between operations  14.1 us (11%)
  Pallas kernels  9.36 us (7%)
  local copies, waits for them, and re-layouts  6.65 us (5%)
    reduce_scatter x1, waiting for transfers between devices, body(): lax.psum_scatter(fields.reshape(NBLK * NBLK, count * BS, 2 * BS), 'sa', s...  44.5 us
    psum x1, blocking collectives, body(): summed = lax.psum(local_sums, 'sa')  30.3 us
    all_to_all x1, starting transfers between devices, body(): tiles = lax.all_to_all(tiles, 'ta', 0, 0, tiled=True)  17.8 us
    pallas_call x1, Pallas kernels, partial_fields(): pl.pallas_call(lambda *refs: fields_kernel(planes, scale, *refs), grid=(m...  9.36 us
    all_to_all x1, waiting for transfers between devices, body(): tiles = lax.all_to_all(tiles, 'ta', 0, 0, tiled=True)  8.33 us
    unnamed x7, local copies, waits for them, and re-layouts  4.9 us
  transfers between devices with their start and end apart: 2, of which 2 were waited for; matrix products, arithmetic and copies ran while one was open for 0% of the time, Pallas kernels for 0%

profile of v2, /device:TPU:1, one launch (start us, length us, event | category | flops | bytes accessed | tf_op | source)
XLA Modules:
  0.0 131.8 jit_solution(5080901118021195090)
XLA Ops:
  7.2 0.0 reduce-scatter.2.cloned.1.call-start
  7.2 0.8 copy.11.refs_1_
  8.0 0.0 copy-start.1
  8.0 1.4 %copy.10 = bf16[1,256,2,3,1,384]{5,1,3,2,4,0:T(8,128)(2,1)S(1)} copy(bf16[1,256,2,3,1,384]{5,2,4,3,1,0:T(2,128)(2,1)} %param.3) | data formatting | bytes 2359296 | tf_op args[0]
  9.4 0.0 copy-done.1
  9.4 9.4 %fields.1 = (f32[16,8,64,128]{3,2,1,0:T(8,128)S(1)}, f32[1,256]{1,0:T(1,128)S(1)}) custom-call(s32[4]{0:T(128)S(1)} %copy-done.1, s32[8,3]{1,0:T(8,128)S(1)} %copy.11.refs_1_, bf16[6,256,384]{2,1,0:T(8,128)(2,1)S(1)} %bitcast.10), custom_call_target="tpu_custom_call" | custom-call | tf_op jit(solution)/shard_map/fields/pallas_call | solution.py:79
  18.8 0.0 copy-start
  18.8 1.9 %copy-done = f32[16,8,64,128]{3,2,1,0:T(8,128)} copy-done((f32[16,8,64,128]{3,2,1,0:T(8,128)}, f32[16,8,64,128]{3,2,1,0:T(8,128)S(1)}, u32[]{:S(2)}) %copy-start) | copy-done | bytes 4194328
  20.7 0.0 reduce-scatter.2.cloned.1.call-update
  20.7 30.3 %psum.7 = f32[1,256]{1,0:T(1,128)S(1)} all-reduce(f32[1,256]{1,0:T(1,128)S(1)} %get-tuple-element.7), channel_id=1, replica_groups=mesh['ta'=32,'sa'=16] {'sa'}, use_global_device_ids=true, to_apply=%region_1.0 | all-reduce | flops 256 | bytes 2048 | tf_op jit(solution)/shard_map/psum | solution.py:115
  51.1 44.5 %reduce-scatter.2.cloned.1.call-done = f32[1,512,128]{2,1,0:T(8,128)} async-done(((f32[16,512,128]{2,1,0:T(8,128)}), f32[1,512,128]{2,1,0:T(8,128)}) %reduce-scatter.2.cloned.1.call-update) | async-done | bytes 262160 | tf_op jit(solution)/shard_map/reduce_scatter | solution.py:112
  95.6 1.7 %copy.12 = f32[32,8,2,128]{3,2,1,0:T(2,128)} copy(f32[32,8,2,128]{3,2,0,1:T(2,128)} %bitcast.13) | data formatting | bytes 524288 | tf_op jit(solution)/shard_map/transpose | solution.py:118
  97.4 17.8 %all-to-all-start = ((f32[32,8,2,128]{3,2,1,0:T(2,128)}), f32[32,8,2,128]{3,2,1,0:T(2,128)S(1)}, u32[]{:S(2)}, u32[]{:S(2)}) async-start(f32[32,8,2,128]{3,2,1,0:T(2,128)} %copy.12), calls=%async_computation.1 | async-start | bytes 524288 | tf_op jit(solution)/shard_map/all_to_all | solution.py:119
  115.2 0.6 broadcast_multiply_fusion
  115.8 8.3 %all-to-all-done = f32[32,8,2,128]{3,2,1,0:T(2,128)S(1)} async-done(((f32[32,8,2,128]{3,2,1,0:T(2,128)}), f32[32,8,2,128]{3,2,1,0:T(2,128)S(1)}, u32[]{:S(2)}, u32[]{:S(2)}) %all-to-all-start) | async-done | bytes 262176 | tf_op jit(solution)/shard_map/all_to_all | solution.py:119
  124.1 0.8 copy.13
Async XLA Ops:
  7.2 88.5 %reduce-scatter.2.cloned.1.call-start = ((), (), s32[]{:S(2)}) async-start(), calls=%async_computation.2 | async-start | bytes 4456448 | tf_op jit(solution)/shard_map/reduce_scatter | solution.py:112
  8.0 1.4 %copy-start.1 = (s32[4]{0:T(128)S(1)}, s32[4]{0:T(128)}, u32[]{:S(2)}) copy-start(s32[4]{0:T(128)} %refs_0_.1) | copy-start | bytes 52
  18.8 1.9 %copy-start = (f32[16,8,64,128]{3,2,1,0:T(8,128)}, f32[16,8,64,128]{3,2,1,0:T(8,128)S(1)}, u32[]{:S(2)}) copy-start(f32[16,8,64,128]{3,2,1,0:T(8,128)S(1)} %get-tuple-element.6) | copy-start | bytes 12582916
  97.4 26.8 %all-to-all-start = ((f32[32,8,2,128]{3,2,1,0:T(2,128)}), f32[32,8,2,128]{3,2,1,0:T(2,128)S(1)}, u32[]{:S(2)}, u32[]{:S(2)}) async-start(f32[32,8,2,128]{3,2,1,0:T(2,128)} %copy.12), calls=%async_computation.1 | async-start | bytes 524288 | tf_op jit(solution)/shard_map/all_to_all | solution.py:119
Sparse Core Ops, SparseCore 0:
  20.9 74.7 reduce-scatter.1

commit v3 on v1

--- a/solution.py
+++ b/solution.py
@@ -103,21 +103,96 @@
     )(block_order, momenta, parts)
 
 
+ROWS = 512
+TAIL = 8
+
+
+def add_kernel(first, toward, hop, nrm_ref, *refs):
+    me = lax.axis_index("sa")
+    peers = lax.axis_size("sa")
+    if first:
+        x_ref, g_ref, out_ref, g_out = refs
+    else:
+        x_ref, g_ref, got_ref, out_ref, g_out = refs
+    owner = lax.rem(me + toward * (peers // 2 - hop) + (0 if toward > 0 else 1) + peers, peers)
+    mine = x_ref[owner]
+    if first:
+        out_ref[pl.ds(0, ROWS)] = mine.reshape(ROWS, 128)
+        out_ref[pl.ds(ROWS, TAIL)] = nrm_ref[...]
+    else:
+        out_ref[pl.ds(0, ROWS)] = mine.reshape(ROWS, 128) + got_ref[pl.ds(0, ROWS)]
+        out_ref[pl.ds(ROWS, TAIL)] = got_ref[pl.ds(ROWS, TAIL)]
+        g_out[hop - 1 + (0 if toward > 0 else 8)] = got_ref[pl.ds(ROWS, TAIL)]
+
+
+def final_kernel(nrm_ref, x_ref, g_ref, r_ref, l_ref, out_ref, nsum_ref, slots):
+    me = lax.axis_index("sa")
+    peers = lax.axis_size("sa")
+    for p in range(8):
+        total = x_ref[me, p] + (r_ref[pl.ds(p * 64, 64)] + l_ref[pl.ds(p * 64, 64)])
+        for r in range(32):
+            out_ref[r, pl.ds(2 * p, 2)] = total[2 * r : 2 * r + 2]
+    slots[me] = nrm_ref[...]
+    for hop in range(8):
+        slots[lax.rem(me - 1 - hop + peers, peers)] = r_ref[pl.ds(ROWS, TAIL)] if hop == 7 else g_ref[hop]
+    for hop in range(7):
+        slots[lax.rem(me + 1 + hop, peers)] = l_ref[pl.ds(ROWS, TAIL)] if hop == 6 else g_ref[8 + hop]
+    total = slots[0]
+    for k in range(1, 16):
+        total = total + slots[k]
+    nsum_ref[...] = total
+
+
+def vm(n):
+    return [pl.BlockSpec(memory_space=pltpu.VMEM)] * n
+
+
+CP = pltpu.CompilerParams(vmem_limit_bytes=40 * 1024 * 1024)
+
+
+def step(toward, hop, nrm, fields, g, got):
+    first = got is None
+    args = (nrm, fields, g) + (() if first else (got,))
+    return pl.pallas_call(
+        lambda *refs: add_kernel(first, toward, hop, *refs),
+        in_specs=vm(len(args)),
+        out_specs=vm(2),
+        out_shape=[jax.ShapeDtypeStruct((ROWS + TAIL, 128), jnp.float32), jax.ShapeDtypeStruct((16, TAIL, 128), jnp.float32)],
+        input_output_aliases={2: 1},
+        compiler_params=CP,
+        name="hop",
+    )(*args)
+
+
 def body(eigenvectors, momenta, block_order):
     planes = eigenvectors.shape[-1]
-    entries = 2 * NC * lax.axis_size("sa") * planes
+    n = lax.axis_size("sa")
+    entries = 2 * NC * n * planes
     parts = jnp.moveaxis(eigenvectors.reshape(NV, PARTS, planes), 1, 0)
-    fields, local_sums = partial_fields(parts, momenta, block_order, 1.0 / math.sqrt(entries))
-    count = momenta.shape[0]
-    owned = lax.psum_scatter(
-        fields.reshape(NBLK * NBLK, count * BS, 2 * BS), "sa", scatter_dimension=0, tiled=True
-    )
-    slice_norms = lax.psum(local_sums, "sa") / entries
-    peers = lax.axis_size("ta")
-    tiles = jnp.moveaxis(owned.reshape(count, peers, BS // peers, 2 * BS), 1, 0)
+    fields, nrm = partial_fields(parts, momenta, block_order, 1.0 / math.sqrt(entries))
+    nrm = jnp.pad(nrm.reshape(2, 128), ((0, 6), (0, 0)))
+    up = [(i, (i + 1) % n) for i in range(n)]
+    down = [(i, (i - 1) % n) for i in range(n)]
+    g = jnp.zeros((16, TAIL, 128), jnp.float32)
+    r = l = None
+    for hop in range(8):
+        send, g = step(1, hop, nrm, fields, g, r)
+        r = lax.ppermute(send, "sa", up)
+        if hop < 7:
+            send, g = step(-1, hop, nrm, fields, g, l)
+            l = lax.ppermute(send, "sa", down)
+    tiles, nsum = pl.pallas_call(
+        final_kernel,
+        in_specs=vm(5),
+        out_specs=vm(2),
+        out_shape=[jax.ShapeDtypeStruct((32, 16, 128), jnp.float32), jax.ShapeDtypeStruct((TAIL, 128), jnp.float32)],
+        scratch_shapes=[pltpu.VMEM((16, TAIL, 128), jnp.float32)],
+        compiler_params=CP,
+        name="final",
+    )(nrm, fields, g, r, l)
     tiles = lax.all_to_all(tiles, "ta", 0, 0, tiled=True)
-    meson_fields = jnp.transpose(tiles, (1, 2, 0, 3))[:, None]
-    return (meson_fields, slice_norms)
+    meson_fields = jnp.transpose(tiles, (1, 0, 2)).reshape(8, 1, 2, 32, 128)
+    return (meson_fields, nsum[:2].reshape(1, NV) / entries)
 
 
 def solution(mesh):

time: 151 us -> 119 us (0.79)
  the two profiles are of different devices: /device:TPU:2 before, /device:TPU:1 now
where the time goes in v3:
time: 119 us; the launch traced here: 118 us
  starting transfers between devices  70.5 us (59%)
  waiting for transfers between devices  33.3 us (28%)
  Pallas kernels  10.7 us (9%)
  local copies, waits for them, and re-layouts  2.32 us (2%)
    ppermute x7, starting transfers between devices, body(): l = lax.ppermute(send, 'sa', down)  36.9 us
    ppermute x8, waiting for transfers between devices, body(): r = lax.ppermute(send, 'sa', up)  24.9 us
    ppermute x8, starting transfers between devices, body(): r = lax.ppermute(send, 'sa', up)  17.8 us
    all_to_all x1, starting transfers between devices, body(): tiles = lax.all_to_all(tiles, 'ta', 0, 0, tiled=True)  15.8 us
    pallas_call x1, Pallas kernels, partial_fields(): pl.pallas_call(lambda *refs: fields_kernel(planes, scale, *refs), grid=(m...  9.34 us
    all_to_all x1, waiting for transfers between devices, body(): tiles = lax.all_to_all(tiles, 'ta', 0, 0, tiled=True)  8.33 us
  transfers between devices with their start and end apart: 16, of which 9 were waited for; matrix products, arithmetic and copies ran while one was open for 0% of the time, Pallas kernels for 0%

profile of v3, /device:TPU:1, one launch (start us, length us, event | category | flops | bytes accessed | tf_op | source)
XLA Modules:
  0.0 118.3 jit_solution(8269413966478130145)
XLA Ops:
  0.6 0.0 copy-start.1
  0.6 0.0 copy-start
  0.6 1.4 %copy.20 = bf16[1,256,2,3,1,384]{5,1,3,2,4,0:T(8,128)(2,1)S(1)} copy(bf16[1,256,2,3,1,384]{5,2,4,3,1,0:T(2,128)(2,1)} %param.3) | data formatting | bytes 2359296 | tf_op args[0]
  2.1 0.0 copy-done.1
  2.1 0.1 copy.21.refs_1_
  2.2 0.0 copy-done
  2.2 9.3 %fields.1 = (f32[16,8,64,128]{3,2,1,0:T(8,128)S(1)}, f32[1,256]{1,0:T(1,128)S(1)}) custom-call(s32[4]{0:T(128)S(1)} %copy-done, s32[8,3]{1,0:T(8,128)S(1)} %copy.21.refs_1_, bf16[6,256,384]{2,1,0:T(8,128)(2,1)S(1)} %bitcast.8), custom_call_target="tpu_custom_call" | custom-call | tf_op jit(solution)/shard_map/fields/pallas_call | solution.py:79
  11.6 4.4 %collective-permute-start = (f32[520,128]{1,0:T(8,128)S(1)}, f32[520,128]{1,0:T(8,128)S(1)}, u32[]{:S(2)}, u32[]{:S(2)}) collective-permute-start(f32[520,128]{1,0:T(8,128)S(1)} %get-tuple-element.40), channel_id=1, source_target_pairs={{0,1},{1,2},{2,3},{3,4},{4,5},{5,6},{6,7},{7,8},{8,9},{9,10},{10,1... | collective-permute-start | bytes 798728 | tf_op jit(solution)/shard_map/ppermute | solution.py:180
  16.0 9.5 %collective-permute-start.1 = (f32[520,128]{1,0:T(8,128)S(1)}, f32[520,128]{1,0:T(8,128)S(1)}, u32[]{:S(2)}, u32[]{:S(2)}) collective-permute-start(f32[520,128]{1,0:T(8,128)S(1)} %get-tuple-element.42), channel_id=1, source_target_pairs={{0,15},{1,0},{2,1},{3,2},{4,3},{5,4},{6,5},{7,6},{8,7},{9,8},{10,9... | collective-permute-start | bytes 798728 | tf_op jit(solution)/shard_map/ppermute | solution.py:183
  25.5 4.1 %collective-permute-done.refs_3_ = f32[520,128]{1,0:T(8,128)S(1)} collective-permute-done((f32[520,128]{1,0:T(8,128)S(1)}, f32[520,128]{1,0:T(8,128)S(1)}, u32[]{:S(2)}, u32[]{:S(2)}) %collective-permute-start) | collective-permute-done | bytes 266272 | tf_op jit(solution)/shard_map/ppermute | solution.py:180
  29.7 1.9 %collective-permute-start.2 = (f32[520,128]{1,0:T(8,128)S(1)}, f32[520,128]{1,0:T(8,128)S(1)}, u32[]{:S(2)}, u32[]{:S(2)}) collective-permute-start(f32[520,128]{1,0:T(8,128)S(1)} %get-tuple-element.44), channel_id=1, source_target_pairs={{0,1},{1,2},{2,3},{3,4},{4,5},{5,6},{6,7},{7,8},{8,9},{9,10},{10,1... | collective-permute-start | bytes 798728 | tf_op jit(solution)/shard_map/ppermute | solution.py:180
  31.6 0.0 collective-permute-done.1.refs_3_
  31.7 4.6 %collective-permute-start.3 = (f32[520,128]{1,0:T(8,128)S(1)}, f32[520,128]{1,0:T(8,128)S(1)}, u32[]{:S(2)}, u32[]{:S(2)}) collective-permute-start(f32[520,128]{1,0:T(8,128)S(1)} %get-tuple-element.46), channel_id=1, source_target_pairs={{0,15},{1,0},{2,1},{3,2},{4,3},{5,4},{6,5},{7,6},{8,7},{9,8},{10,9... | collective-permute-start | bytes 798728 | tf_op jit(solution)/shard_map/ppermute | solution.py:183
  36.2 3.2 %collective-permute-done.2.refs_3_ = f32[520,128]{1,0:T(8,128)S(1)} collective-permute-done((f32[520,128]{1,0:T(8,128)S(1)}, f32[520,128]{1,0:T(8,128)S(1)}, u32[]{:S(2)}, u32[]{:S(2)}) %collective-permute-start.2) | collective-permute-done | bytes 266272 | tf_op jit(solution)/shard_map/ppermute | solution.py:180
  39.5 1.9 %collective-permute-start.4 = (f32[520,128]{1,0:T(8,128)S(1)}, f32[520,128]{1,0:T(8,128)S(1)}, u32[]{:S(2)}, u32[]{:S(2)}) collective-permute-start(f32[520,128]{1,0:T(8,128)S(1)} %get-tuple-element.48), channel_id=1, source_target_pairs={{0,1},{1,2},{2,3},{3,4},{4,5},{5,6},{6,7},{7,8},{8,9},{9,10},{10,1... | collective-permute-start | bytes 798728 | tf_op jit(solution)/shard_map/ppermute | solution.py:180
  41.4 0.0 collective-permute-done.3.refs_3_
  41.5 4.6 %collective-permute-start.5 = (f32[520,128]{1,0:T(8,128)S(1)}, f32[520,128]{1,0:T(8,128)S(1)}, u32[]{:S(2)}, u32[]{:S(2)}) collective-permute-start(f32[520,128]{1,0:T(8,128)S(1)} %get-tuple-element.50), channel_id=1, source_target_pairs={{0,15},{1,0},{2,1},{3,2},{4,3},{5,4},{6,5},{7,6},{8,7},{9,8},{10,9... | collective-permute-start | bytes 798728 | tf_op jit(solution)/shard_map/ppermute | solution.py:183
  46.0 2.3 %collective-permute-done.4.refs_3_ = f32[520,128]{1,0:T(8,128)S(1)} collective-permute-done((f32[520,128]{1,0:T(8,128)S(1)}, f32[520,128]{1,0:T(8,128)S(1)}, u32[]{:S(2)}, u32[]{:S(2)}) %collective-permute-start.4) | collective-permute-done | bytes 266272 | tf_op jit(solution)/shard_map/ppermute | solution.py:180
  48.3 1.9 %collective-permute-start.6 = (f32[520,128]{1,0:T(8,128)S(1)}, f32[520,128]{1,0:T(8,128)S(1)}, u32[]{:S(2)}, u32[]{:S(2)}) collective-permute-start(f32[520,128]{1,0:T(8,128)S(1)} %get-tuple-element.52), channel_id=1, source_target_pairs={{0,1},{1,2},{2,3},{3,4},{4,5},{5,6},{6,7},{7,8},{8,9},{9,10},{10,1... | collective-permute-start | bytes 798728 | tf_op jit(solution)/shard_map/ppermute | solution.py:180
  50.3 0.0 collective-permute-done.5.refs_3_
  50.3 4.6 %collective-permute-start.7 = (f32[520,128]{1,0:T(8,128)S(1)}, f32[520,128]{1,0:T(8,128)S(1)}, u32[]{:S(2)}, u32[]{:S(2)}) collective-permute-start(f32[520,128]{1,0:T(8,128)S(1)} %get-tuple-element.54), channel_id=1, source_target_pairs={{0,15},{1,0},{2,1},{3,2},{4,3},{5,4},{6,5},{7,6},{8,7},{9,8},{10,9... | collective-permute-start | bytes 798728 | tf_op jit(solution)/shard_map/ppermute | solution.py:183
  54.9 1.8 %collective-permute-done.6.refs_3_ = f32[520,128]{1,0:T(8,128)S(1)} collective-permute-done((f32[520,128]{1,0:T(8,128)S(1)}, f32[520,128]{1,0:T(8,128)S(1)}, u32[]{:S(2)}, u32[]{:S(2)}) %collective-permute-start.6) | collective-permute-done | bytes 266272 | tf_op jit(solution)/shard_map/ppermute | solution.py:180
  56.7 1.9 %collective-permute-start.8 = (f32[520,128]{1,0:T(8,128)S(1)}, f32[520,128]{1,0:T(8,128)S(1)}, u32[]{:S(2)}, u32[]{:S(2)}) collective-permute-start(f32[520,128]{1,0:T(8,128)S(1)} %get-tuple-element.56), channel_id=1, source_target_pairs={{0,1},{1,2},{2,3},{3,4},{4,5},{5,6},{6,7},{7,8},{8,9},{9,10},{10,1... | collective-permute-start | bytes 798728 | tf_op jit(solution)/shard_map/ppermute | solution.py:180
  58.7 0.0 collective-permute-done.7.refs_3_
  58.7 4.6 %collective-permute-start.9 = (f32[520,128]{1,0:T(8,128)S(1)}, f32[520,128]{1,0:T(8,128)S(1)}, u32[]{:S(2)}, u32[]{:S(2)}) collective-permute-start(f32[520,128]{1,0:T(8,128)S(1)} %get-tuple-element.58), channel_id=1, source_target_pairs={{0,15},{1,0},{2,1},{3,2},{4,3},{5,4},{6,5},{7,6},{8,7},{9,8},{10,9... | collective-permute-start | bytes 798728 | tf_op jit(solution)/shard_map/ppermute | solution.py:183
  63.3 1.8 %collective-permute-done.8.refs_3_ = f32[520,128]{1,0:T(8,128)S(1)} collective-permute-done((f32[520,128]{1,0:T(8,128)S(1)}, f32[520,128]{1,0:T(8,128)S(1)}, u32[]{:S(2)}, u32[]{:S(2)}) %collective-permute-start.8) | collective-permute-done | bytes 266272 | tf_op jit(solution)/shard_map/ppermute | solution.py:180
  65.2 1.9 %collective-permute-start.10 = (f32[520,128]{1,0:T(8,128)S(1)}, f32[520,128]{1,0:T(8,128)S(1)}, u32[]{:S(2)}, u32[]{:S(2)}) collective-permute-start(f32[520,128]{1,0:T(8,128)S(1)} %get-tuple-element.60), channel_id=1, source_target_pairs={{0,1},{1,2},{2,3},{3,4},{4,5},{5,6},{6,7},{7,8},{8,9},{9,10},{10,1... | collective-permute-start | bytes 798728 | tf_op jit(solution)/shard_map/ppermute | solution.py:180
  67.1 0.0 collective-permute-done.9.refs_3_
  67.1 4.6 %collective-permute-start.11 = (f32[520,128]{1,0:T(8,128)S(1)}, f32[520,128]{1,0:T(8,128)S(1)}, u32[]{:S(2)}, u32[]{:S(2)}) collective-permute-start(f32[520,128]{1,0:T(8,128)S(1)} %get-tuple-element.62), channel_id=1, source_target_pairs={{0,15},{1,0},{2,1},{3,2},{4,3},{5,4},{6,5},{7,6},{8,7},{9,8},{10,9... | collective-permute-start | bytes 798728 | tf_op jit(solution)/shard_map/ppermute | solution.py:183
  71.7 1.8 %collective-permute-done.10.refs_3_ = f32[520,128]{1,0:T(8,128)S(1)} collective-permute-done((f32[520,128]{1,0:T(8,128)S(1)}, f32[520,128]{1,0:T(8,128)S(1)}, u32[]{:S(2)}, u32[]{:S(2)}) %collective-permute-start.10) | collective-permute-done | bytes 266272 | tf_op jit(solution)/shard_map/ppermute | solution.py:180
  73.6 1.9 %collective-permute-start.12 = (f32[520,128]{1,0:T(8,128)S(1)}, f32[520,128]{1,0:T(8,128)S(1)}, u32[]{:S(2)}, u32[]{:S(2)}) collective-permute-start(f32[520,128]{1,0:T(8,128)S(1)} %get-tuple-element.64), channel_id=1, source_target_pairs={{0,1},{1,2},{2,3},{3,4},{4,5},{5,6},{6,7},{7,8},{8,9},{9,10},{10,1... | collective-permute-start | bytes 798728 | tf_op jit(solution)/shard_map/ppermute | solution.py:180
  75.5 0.0 collective-permute-done.11.refs_3_
  75.5 4.6 %collective-permute-start.14 = (f32[520,128]{1,0:T(8,128)S(1)}, f32[520,128]{1,0:T(8,128)S(1)}, u32[]{:S(2)}, u32[]{:S(2)}) collective-permute-start(f32[520,128]{1,0:T(8,128)S(1)} %get-tuple-element.67), channel_id=1, source_target_pairs={{0,15},{1,0},{2,1},{3,2},{4,3},{5,4},{6,5},{7,6},{8,7},{9,8},{10,9... | collective-permute-start | bytes 798728 | tf_op jit(solution)/shard_map/ppermute | solution.py:183
  80.1 2.1 %collective-permute-done.12.refs_3_ = f32[520,128]{1,0:T(8,128)S(1)} collective-permute-done((f32[520,128]{1,0:T(8,128)S(1)}, f32[520,128]{1,0:T(8,128)S(1)}, u32[]{:S(2)}, u32[]{:S(2)}) %collective-permute-start.12) | collective-permute-done | bytes 266272 | tf_op jit(solution)/shard_map/ppermute | solution.py:180
  82.3 1.9 %collective-permute-start.13 = (f32[520,128]{1,0:T(8,128)S(1)}, f32[520,128]{1,0:T(8,128)S(1)}, u32[]{:S(2)}, u32[]{:S(2)}) collective-permute-start(f32[520,128]{1,0:T(8,128)S(1)} %get-tuple-element.66), channel_id=1, source_target_pairs={{0,1},{1,2},{2,3},{3,4},{4,5},{5,6},{6,7},{7,8},{8,9},{9,10},{10,1... | collective-permute-start | bytes 798728 | tf_op jit(solution)/shard_map/ppermute | solution.py:180
  84.2 0.0 collective-permute-done.14.l_ref
  84.2 7.8 %collective-permute-done.13.r_ref = f32[520,128]{1,0:T(8,128)S(1)} collective-permute-done((f32[520,128]{1,0:T(8,128)S(1)}, f32[520,128]{1,0:T(8,128)S(1)}, u32[]{:S(2)}, u32[]{:S(2)}) %collective-permute-start.13) | collective-permute-done | bytes 266272 | tf_op jit(solution)/shard_map/ppermute | solution.py:180
  92.0 0.8 final.1
  92.8 15.8 %all-to-all-start = ((f32[32,16,128]{2,1,0:T(8,128)}), f32[32,16,128]{2,1,0:T(8,128)S(1)}, u32[]{:S(2)}, u32[]{:S(2)}) async-start(f32[32,16,128]{2,1,0:T(8,128)} %get-tuple-element.68), calls=%async_computation | async-start | bytes 524288 | tf_op jit(solution)/shard_map/all_to_all | solution.py:193
  108.6 0.6 slice_multiply_fusion
  109.2 8.3 %all-to-all-done = f32[32,16,128]{2,1,0:T(8,128)S(1)} async-done(((f32[32,16,128]{2,1,0:T(8,128)}), f32[32,16,128]{2,1,0:T(8,128)S(1)}, u32[]{:S(2)}, u32[]{:S(2)}) %all-to-all-start) | async-done | bytes 262176 | tf_op jit(solution)/shard_map/all_to_all | solution.py:193
  117.5 0.8 copy.22
  (17 shorter events, 0.5 us)
Async XLA Ops:
  0.6 1.5 %copy-start.1 = (s32[8,3]{0,1:T(4,128)S(1)}, s32[8,3]{0,1:T(4,128)}, u32[]{:S(2)}) copy-start(s32[8,3]{0,1:T(4,128)} %param.4) | copy-start | bytes 292
  0.6 1.5 %copy-start = (s32[4]{0:T(128)S(1)}, s32[4]{0:T(128)}, u32[]{:S(2)}) copy-start(s32[4]{0:T(128)} %refs_0_.1) | copy-start | bytes 52
  11.6 18.1 %collective-permute-start = (f32[520,128]{1,0:T(8,128)S(1)}, f32[520,128]{1,0:T(8,128)S(1)}, u32[]{:S(2)}, u32[]{:S(2)}) collective-permute-start(f32[520,128]{1,0:T(8,128)S(1)} %get-tuple-element.40), channel_id=1, source_target_pairs={{0,1},{1,2},{2,3},{3,4},{4,5},{5,6},{6,7},{7,8},{8,9},{9,10},{10,1... | collective-permute-start | bytes 798728 | tf_op jit(solution)/shard_map/ppermute | solution.py:180
  16.0 15.6 %collective-permute-start.1 = (f32[520,128]{1,0:T(8,128)S(1)}, f32[520,128]{1,0:T(8,128)S(1)}, u32[]{:S(2)}, u32[]{:S(2)}) collective-permute-start(f32[520,128]{1,0:T(8,128)S(1)} %get-tuple-element.42), channel_id=1, source_target_pairs={{0,15},{1,0},{2,1},{3,2},{4,3},{5,4},{6,5},{7,6},{8,7},{9,8},{10,9... | collective-permute-start | bytes 798728 | tf_op jit(solution)/shard_map/ppermute | solution.py:183
  29.7 9.8 %collective-permute-start.2 = (f32[520,128]{1,0:T(8,128)S(1)}, f32[520,128]{1,0:T(8,128)S(1)}, u32[]{:S(2)}, u32[]{:S(2)}) collective-permute-start(f32[520,128]{1,0:T(8,128)S(1)} %get-tuple-element.44), channel_id=1, source_target_pairs={{0,1},{1,2},{2,3},{3,4},{4,5},{5,6},{6,7},{7,8},{8,9},{9,10},{10,1... | collective-permute-start | bytes 798728 | tf_op jit(solution)/shard_map/ppermute | solution.py:180
  31.7 9.7 %collective-permute-start.3 = (f32[520,128]{1,0:T(8,128)S(1)}, f32[520,128]{1,0:T(8,128)S(1)}, u32[]{:S(2)}, u32[]{:S(2)}) collective-permute-start(f32[520,128]{1,0:T(8,128)S(1)} %get-tuple-element.46), channel_id=1, source_target_pairs={{0,15},{1,0},{2,1},{3,2},{4,3},{5,4},{6,5},{7,6},{8,7},{9,8},{10,9... | collective-permute-start | bytes 798728 | tf_op jit(solution)/shard_map/ppermute | solution.py:183
  39.5 8.8 %collective-permute-start.4 = (f32[520,128]{1,0:T(8,128)S(1)}, f32[520,128]{1,0:T(8,128)S(1)}, u32[]{:S(2)}, u32[]{:S(2)}) collective-permute-start(f32[520,128]{1,0:T(8,128)S(1)} %get-tuple-element.48), channel_id=1, source_target_pairs={{0,1},{1,2},{2,3},{3,4},{4,5},{5,6},{6,7},{7,8},{8,9},{9,10},{10,1... | collective-permute-start | bytes 798728 | tf_op jit(solution)/shard_map/ppermute | solution.py:180
  41.5 8.8 %collective-permute-start.5 = (f32[520,128]{1,0:T(8,128)S(1)}, f32[520,128]{1,0:T(8,128)S(1)}, u32[]{:S(2)}, u32[]{:S(2)}) collective-permute-start(f32[520,128]{1,0:T(8,128)S(1)} %get-tuple-element.50), channel_id=1, source_target_pairs={{0,15},{1,0},{2,1},{3,2},{4,3},{5,4},{6,5},{7,6},{8,7},{9,8},{10,9... | collective-permute-start | bytes 798728 | tf_op jit(solution)/shard_map/ppermute | solution.py:183
  48.3 8.4 %collective-permute-start.6 = (f32[520,128]{1,0:T(8,128)S(1)}, f32[520,128]{1,0:T(8,128)S(1)}, u32[]{:S(2)}, u32[]{:S(2)}) collective-permute-start(f32[520,128]{1,0:T(8,128)S(1)} %get-tuple-element.52), channel_id=1, source_target_pairs={{0,1},{1,2},{2,3},{3,4},{4,5},{5,6},{6,7},{7,8},{8,9},{9,10},{10,1... | collective-permute-start | bytes 798728 | tf_op jit(solution)/shard_map/ppermute | solution.py:180
  50.3 8.4 %collective-permute-start.7 = (f32[520,128]{1,0:T(8,128)S(1)}, f32[520,128]{1,0:T(8,128)S(1)}, u32[]{:S(2)}, u32[]{:S(2)}) collective-permute-start(f32[520,128]{1,0:T(8,128)S(1)} %get-tuple-element.54), channel_id=1, source_target_pairs={{0,15},{1,0},{2,1},{3,2},{4,3},{5,4},{6,5},{7,6},{8,7},{9,8},{10,9... | collective-permute-start | bytes 798728 | tf_op jit(solution)/shard_map/ppermute | solution.py:183
  56.7 8.4 %collective-permute-start.8 = (f32[520,128]{1,0:T(8,128)S(1)}, f32[520,128]{1,0:T(8,128)S(1)}, u32[]{:S(2)}, u32[]{:S(2)}) collective-permute-start(f32[520,128]{1,0:T(8,128)S(1)} %get-tuple-element.56), channel_id=1, source_target_pairs={{0,1},{1,2},{2,3},{3,4},{4,5},{5,6},{6,7},{7,8},{8,9},{9,10},{10,1... | collective-permute-start | bytes 798728 | tf_op jit(solution)/shard_map/ppermute | solution.py:180
  58.7 8.4 %collective-permute-start.9 = (f32[520,128]{1,0:T(8,128)S(1)}, f32[520,128]{1,0:T(8,128)S(1)}, u32[]{:S(2)}, u32[]{:S(2)}) collective-permute-start(f32[520,128]{1,0:T(8,128)S(1)} %get-tuple-element.58), channel_id=1, source_target_pairs={{0,15},{1,0},{2,1},{3,2},{4,3},{5,4},{6,5},{7,6},{8,7},{9,8},{10,9... | collective-permute-start | bytes 798728 | tf_op jit(solution)/shard_map/ppermute | solution.py:183
  65.2 8.4 %collective-permute-start.10 = (f32[520,128]{1,0:T(8,128)S(1)}, f32[520,128]{1,0:T(8,128)S(1)}, u32[]{:S(2)}, u32[]{:S(2)}) collective-permute-start(f32[520,128]{1,0:T(8,128)S(1)} %get-tuple-element.60), channel_id=1, source_target_pairs={{0,1},{1,2},{2,3},{3,4},{4,5},{5,6},{6,7},{7,8},{8,9},{9,10},{10,1... | collective-permute-start | bytes 798728 | tf_op jit(solution)/shard_map/ppermute | solution.py:180
  67.1 8.4 %collective-permute-start.11 = (f32[520,128]{1,0:T(8,128)S(1)}, f32[520,128]{1,0:T(8,128)S(1)}, u32[]{:S(2)}, u32[]{:S(2)}) collective-permute-start(f32[520,128]{1,0:T(8,128)S(1)} %get-tuple-element.62), channel_id=1, source_target_pairs={{0,15},{1,0},{2,1},{3,2},{4,3},{5,4},{6,5},{7,6},{8,7},{9,8},{10,9... | collective-permute-start | bytes 798728 | tf_op jit(solution)/shard_map/ppermute | solution.py:183
  73.6 8.7 %collective-permute-start.12 = (f32[520,128]{1,0:T(8,128)S(1)}, f32[520,128]{1,0:T(8,128)S(1)}, u32[]{:S(2)}, u32[]{:S(2)}) collective-permute-start(f32[520,128]{1,0:T(8,128)S(1)} %get-tuple-element.64), channel_id=1, source_target_pairs={{0,1},{1,2},{2,3},{3,4},{4,5},{5,6},{6,7},{7,8},{8,9},{9,10},{10,1... | collective-permute-start | bytes 798728 | tf_op jit(solution)/shard_map/ppermute | solution.py:180
  75.5 8.6 %collective-permute-start.14 = (f32[520,128]{1,0:T(8,128)S(1)}, f32[520,128]{1,0:T(8,128)S(1)}, u32[]{:S(2)}, u32[]{:S(2)}) collective-permute-start(f32[520,128]{1,0:T(8,128)S(1)} %get-tuple-element.67), channel_id=1, source_target_pairs={{0,15},{1,0},{2,1},{3,2},{4,3},{5,4},{6,5},{7,6},{8,7},{9,8},{10,9... | collective-permute-start | bytes 798728 | tf_op jit(solution)/shard_map/ppermute | solution.py:183
  82.3 9.7 %collective-permute-start.13 = (f32[520,128]{1,0:T(8,128)S(1)}, f32[520,128]{1,0:T(8,128)S(1)}, u32[]{:S(2)}, u32[]{:S(2)}) collective-permute-start(f32[520,128]{1,0:T(8,128)S(1)} %get-tuple-element.66), channel_id=1, source_target_pairs={{0,1},{1,2},{2,3},{3,4},{4,5},{5,6},{6,7},{7,8},{8,9},{9,10},{10,1... | collective-permute-start | bytes 798728 | tf_op jit(solution)/shard_map/ppermute | solution.py:180
  92.8 24.7 %all-to-all-start = ((f32[32,16,128]{2,1,0:T(8,128)}), f32[32,16,128]{2,1,0:T(8,128)S(1)}, u32[]{:S(2)}, u32[]{:S(2)}) async-start(f32[32,16,128]{2,1,0:T(8,128)} %get-tuple-element.68), calls=%async_computation | async-start | bytes 524288 | tf_op jit(solution)/shard_map/all_to_all | solution.py:193

commit v4 on v3

v4 whole, which is shorter than its diff:
```python
import math

import jax
import jax.numpy as jnp
from jax import lax
from jax.experimental import pallas as pl
from jax.experimental.pallas import tpu as pltpu
from jax.sharding import PartitionSpec as P

NC = 3
BS = 64
NBLK = 4
NV = NBLK * BS
LX = 96
PARTS = 2 * NC
full_turn = 2.0 * math.pi


def near_columns():
    first = lax.rem(lax.axis_index("sa") + lax.axis_size("sa") // 2, NBLK)
    columns = [lax.rem(first + k, NBLK) for k in range(NBLK)]
    return columns[:2], columns[2:]


def fill_left(order_ref, x_ref, left_ref):
    planes = x_ref.shape[-1]
    half = NC * planes
    for k in range(NBLK):
        stored = pl.ds(pl.multiple_of(order_ref[k] * BS, BS), BS)
        for c in range(NC):
            re = x_ref[c, stored, :]
            im = x_ref[NC + c, stored, :]
            lanes, after = pl.ds(c * planes, planes), pl.ds(half + c * planes, planes)
            left_ref[pl.ds(2 * k * BS, BS), lanes] = re
            left_ref[pl.ds(2 * k * BS, BS), after] = im
            left_ref[pl.ds((2 * k + 1) * BS, BS), lanes] = -im
            left_ref[pl.ds((2 * k + 1) * BS, BS), after] = re


def fill_right(n, b, count, order_ref, x_ref, cosines, sines, right_ref):
    planes = x_ref.shape[-1]
    half = NC * planes
    stored = pl.ds(pl.multiple_of(order_ref[b] * BS, BS), BS)
    for c in range(NC):
        re = x_ref[c, stored, :].astype(jnp.float32)
        im = x_ref[NC + c, stored, :].astype(jnp.float32)
        for p in range(count):
            cos = cosines[p : p + 1]
            sin = sines[p : p + 1]
            rows = pl.ds((n * count + p) * BS, BS)
            right_ref[rows, pl.ds(c * planes, planes)] = (re * cos + im * sin).astype(jnp.bfloat16)
            right_ref[rows, pl.ds(half + c * planes, planes)] = (im * cos - re * sin).astype(jnp.bfloat16)


def multiply(columns, scale, order_ref, x_ref, cosines, sines, right_ref, left_ref, out_ref):
    count = cosines.shape[0]
    size = count * BS
    for n, b in enumerate(columns):
        fill_right(n, b, count, order_ref, x_ref, cosines, sines, right_ref)
    product = lax.dot_general(
        right_ref[...], left_ref[...], (((1,), (1,)), ((), ())), preferred_element_type=jnp.float32
    )
    product = product * scale
    for n, b in enumerate(columns):
        for a in range(NBLK):
            cut = product[n * size : (n + 1) * size, a * 2 * BS : (a + 1) * 2 * BS]
            out_ref[a * NBLK + b] = cut.reshape(count, BS, 2 * BS)


def first_kernel(scale, order_ref, mom_ref, x_ref, out_ref, nrm_ref, left_ref, cos_ref, sin_ref, right_ref):
    planes = x_ref.shape[-1]
    count = mom_ref.shape[1]
    site = lax.broadcasted_iota(jnp.int32, (count, planes), 1).astype(jnp.float32)
    y = jnp.floor((site + 0.5) * (1.0 / LX))
    x = site - LX * y
    z = lax.axis_index("sa").astype(jnp.float32)
    which = lax.broadcasted_iota(jnp.int32, (count, planes), 0)
    mom = [jnp.zeros((count, planes), jnp.float32)] * 3
    for p in range(count):
        mom = [jnp.where(which == p, mom_ref[k, p].astype(jnp.float32), mom[k]) for k in range(3)]
    index = mom[0] * x + mom[1] * y + mom[2] * z
    index = index - LX * jnp.floor((index + 0.5) * (1.0 / LX))
    angles = index * (full_turn / LX)
    cosines = jnp.cos(angles)
    sines = jnp.sin(angles)
    cos_ref[...] = cosines
    sin_ref[...] = sines
    fill_left(order_ref, x_ref, left_ref)
    multiply(near_columns()[0], scale, order_ref, x_ref, cosines, sines, right_ref, left_ref, out_ref)
    squares = jnp.zeros((NV, 128), jnp.float32)
    for k in range(PARTS):
        for l in range(planes // 128):
            v = x_ref[k, :, pl.ds(l * 128, 128)].astype(jnp.float32)
            squares = squares + v * v
    sums = jnp.sum(squares.T, axis=0, keepdims=True)
    nrm_ref[...] = jnp.zeros(nrm_ref.shape, jnp.float32)
    for k in range(NV // 128):
        nrm_ref[pl.ds(k, 1)] = sums[:, k * 128 : (k + 1) * 128]


def second_kernel(scale, order_ref, x_ref, cos_ref, sin_ref, left_ref, made_ref, after_ref, out_ref, right_ref):
    multiply(near_columns()[1], scale, order_ref, x_ref, cos_ref[...], sin_ref[...], right_ref, left_ref, out_ref)


def first_half(parts, momenta, block_order, scale):
    planes = parts.shape[-1]
    count = momenta.shape[0]
    depth = PARTS * planes
    return pl.pallas_call(
        lambda *refs: first_kernel(scale, *refs),
        in_specs=[pl.BlockSpec(memory_space=pltpu.SMEM)] * 2 + vm(1),
        out_specs=vm(5),
        out_shape=[
            jax.ShapeDtypeStruct((NBLK * NBLK, count, BS, 2 * BS), jnp.float32),
            jax.ShapeDtypeStruct((TAIL, 128), jnp.float32),
            jax.ShapeDtypeStruct((2 * NV, depth), jnp.bfloat16),
            jax.ShapeDtypeStruct((count, planes), jnp.float32),
            jax.ShapeDtypeStruct((count, planes), jnp.float32),
        ],
        scratch_shapes=[pltpu.VMEM((count * 2 * BS, depth), jnp.bfloat16)],
        compiler_params=CP,
        name="fields_first",
    )(block_order, momenta.T, parts)


def second_half(parts, block_order, made, after, scale):
    fields, _, left, cosines, sines = made
    return pl.pallas_call(
        lambda *refs: second_kernel(scale, *refs),
        in_specs=[pl.BlockSpec(memory_space=pltpu.SMEM)] + vm(5) + [pl.BlockSpec(memory_space=pl.ANY)],
        out_specs=vm(1)[0],
        out_shape=jax.ShapeDtypeStruct(fields.shape, jnp.float32),
        input_output_aliases={5: 0},
        scratch_shapes=[pltpu.VMEM((cosines.shape[0] * 2 * BS, left.shape[1]), jnp.bfloat16)],
        compiler_params=CP,
        name="fields_second",
    )(block_order, parts, cosines, sines, left, fields, after)


ROWS = 512
TAIL = 8


def add_kernel(first, toward, hop, nrm_ref, *refs):
    me = lax.axis_index("sa")
    peers = lax.axis_size("sa")
    if first:
        x_ref, g_ref, out_ref, g_out = refs
    else:
        x_ref, g_ref, got_ref, out_ref, g_out = refs
    owner = lax.rem(me + toward * (peers // 2 - hop) + (0 if toward > 0 else 1) + peers, peers)
    mine = x_ref[owner]
    if first:
        out_ref[pl.ds(0, ROWS)] = mine.reshape(ROWS, 128)
        out_ref[pl.ds(ROWS, TAIL)] = nrm_ref[...]
    else:
        out_ref[pl.ds(0, ROWS)] = mine.reshape(ROWS, 128) + got_ref[pl.ds(0, ROWS)]
        out_ref[pl.ds(ROWS, TAIL)] = got_ref[pl.ds(ROWS, TAIL)]
        g_out[hop - 1 + (0 if toward > 0 else 8)] = got_ref[pl.ds(ROWS, TAIL)]


def final_kernel(entries, nrm_ref, x_ref, g_ref, r_ref, l_ref, out_ref, nsum_ref, slots):
    me = lax.axis_index("sa")
    peers = lax.axis_size("sa")
    low = lax.broadcasted_iota(jnp.int32, (BS, 2 * BS), 1) < BS
    for p in range(0, 8, 2):
        rows = pl.ds(p * BS, 2 * BS)
        total = x_ref[me, pl.ds(p, 2)].reshape(2 * BS, 2 * BS) + (r_ref[rows] + l_ref[rows])
        turned = total.T
        real, imag = turned[:BS], turned[BS:]
        for k, tile in enumerate(
            (jnp.where(low, real, pltpu.roll(imag, BS, 1)), jnp.where(low, pltpu.roll(real, BS, 1), imag))
        ):
            for r in range(32):
                out_ref[r, pl.ds(2 * (p + k), 2)] = tile[2 * r : 2 * r + 2]
    slots[me] = nrm_ref[...]
    for hop in range(8):
        slots[lax.rem(me - 1 - hop + peers, peers)] = r_ref[pl.ds(ROWS, TAIL)] if hop == 7 else g_ref[hop]
    for hop in range(7):
        slots[lax.rem(me + 1 + hop, peers)] = l_ref[pl.ds(ROWS, TAIL)] if hop == 6 else g_ref[8 + hop]
    total = slots[0]
    for k in range(1, 16):
        total = total + slots[k]
    for k in range(NV // 128):
        nsum_ref[:, pl.ds(k * 128, 128)] = total[k : k + 1] / entries


def vm(n):
    return [pl.BlockSpec(memory_space=pltpu.VMEM)] * n


CP = pltpu.CompilerParams(vmem_limit_bytes=40 * 1024 * 1024)


def step(toward, hop, nrm, fields, g, got):
    first = got is None
    args = (nrm, fields, g) + (() if first else (got,))
    return pl.pallas_call(
        lambda *refs: add_kernel(first, toward, hop, *refs),
        in_specs=vm(len(args)),
        out_specs=vm(2),
        out_shape=[jax.ShapeDtypeStruct((ROWS + TAIL, 128), jnp.float32), jax.ShapeDtypeStruct((16, TAIL, 128), jnp.float32)],
        input_output_aliases={2: 1},
        compiler_params=CP,
        name="hop",
    )(*args)


def body(eigenvectors, momenta, block_order):
    planes = eigenvectors.shape[-1]
    n = lax.axis_size("sa")
    entries = 2 * NC * n * planes
    parts = jnp.moveaxis(eigenvectors.reshape(NV, PARTS, planes), 1, 0)
    scale = 1.0 / math.sqrt(entries)
    made = first_half(parts, momenta, block_order, scale)
    fields, nrm = made[:2]
    up = [(i, (i + 1) % n) for i in range(n)]
    down = [(i, (i - 1) % n) for i in range(n)]
    g = jnp.zeros((16, TAIL, 128), jnp.float32)
    r = l = None
    for hop in range(8):
        send, g = step(1, hop, nrm, fields, g, r)
        r = lax.ppermute(send, "sa", up)
        if hop < 7:
            send, g = step(-1, hop, nrm, fields, g, l)
            l = lax.ppermute(send, "sa", down)
        if hop == 0:
            fields = second_half(parts, block_order, made, g, scale)
    tiles, nsum = pl.pallas_call(
        lambda *refs: final_kernel(entries, *refs),
        in_specs=vm(5),
        out_specs=vm(2),
        out_shape=[jax.ShapeDtypeStruct((32, 16, 128), jnp.float32), jax.ShapeDtypeStruct((1, NV), jnp.float32)],
        scratch_shapes=[pltpu.VMEM((16, TAIL, 128), jnp.float32)],
        compiler_params=CP,
        name="final",
    )(nrm, fields, g, r, l)
    tiles = lax.all_to_all(tiles, "ta", 0, 0, tiled=True)
    meson_fields = jnp.transpose(tiles, (1, 0, 2)).reshape(8, 1, 2, 32, 128)
    return (meson_fields, nsum)


def solution(mesh):
    return jax.shard_map(
        body,
        mesh=mesh,
        in_specs=(P("ta", None, None, None, "sa", None), P(), P()),
        out_specs=(P(None, "sa", "ta", None, None), P("ta", None)),
        check_vma=False,
    )
```

time: 119 us -> 113 us (0.950)
  blocking collectives: 0 us -> 24.4 us
  starting transfers between devices: 70.5 us -> 54.8 us
  waiting for transfers between devices: 33.3 us -> 21.7 us
  Pallas kernels: 10.7 us -> 8.05 us
    all_to_all x0 -> x1, blocking collectives: none -> 24.4 us  [body(): tiles = lax.all_to_all(tiles, 'ta', 0, 0, tiled=True)]
    all_to_all x1 -> x0, starting transfers between devices: 15.8 us -> none  [body(): tiles = lax.all_to_all(tiles, 'ta', 0, 0, tiled=True)]
    all_to_all x1 -> x0, waiting for transfers between devices: 8.33 us -> none  [body(): tiles = lax.all_to_all(tiles, 'ta', 0, 0, tiled=True)]
    ppermute x8, waiting for transfers between devices: 24.9 us -> 21.6 us  [body(): r = lax.ppermute(send, 'sa', up)]
    pallas_call x2 -> x3, Pallas kernels: 10.1 us -> 7.54 us  [the longest x1 3.49 us: first_half(): pl.pallas_call(lambda *refs: first_kernel(scale, *refs), in_specs=[pl.Blo...]
  transfers between devices with their start and end apart: 16 -> 15, of which waited for: 9 -> 8; matrix products, arithmetic and copies ran while one was open for 0% -> 0% of each run, Pallas kernels for 0% -> 3%
where the time goes in v4:
time: 113 us; the launch traced here: 112 us
  starting transfers between devices  54.8 us (48%)
  blocking collectives  24.4 us (22%)
  waiting for transfers between devices  21.7 us (19%)
  Pallas kernels  8.05 us (7%)
  local copies, waits for them, and re-layouts  2.23 us (2%)
    ppermute x7, starting transfers between devices, body(): l = lax.ppermute(send, 'sa', down)  37 us
    all_to_all x1, blocking collectives, body(): tiles = lax.all_to_all(tiles, 'ta', 0, 0, tiled=True)  24.4 us
    ppermute x8, waiting for transfers between devices, body(): r = lax.ppermute(send, 'sa', up)  21.6 us
    ppermute x8, starting transfers between devices, body(): r = lax.ppermute(send, 'sa', up)  17.8 us
    pallas_call x1, Pallas kernels, first_half(): pl.pallas_call(lambda *refs: first_kernel(scale, *refs), in_specs=[pl.Blo...  3.49 us
    pallas_call x1, Pallas kernels, second_half(): pl.pallas_call(lambda *refs: second_kernel(scale, *refs), in_specs=[pl.Bl...  3.24 us
  transfers between devices with their start and end apart: 15, of which 8 were waited for; matrix products, arithmetic and copies ran while one was open for 0% of the time, Pallas kernels for 3%

profile of v4, /device:TPU:1, one launch (start us, length us, event | category | flops | bytes accessed | tf_op | source)
XLA Modules:
  0.0 112.1 jit_solution(12241689087411776902)
XLA Ops:
  0.6 0.0 copy-start.1
  0.6 0.0 copy-start
  0.6 1.4 %copy.21 = bf16[1,256,2,3,1,384]{5,1,3,2,4,0:T(8,128)(2,1)S(1)} copy(bf16[1,256,2,3,1,384]{5,2,4,3,1,0:T(2,128)(2,1)} %param.3) | data formatting | bytes 2359296 | tf_op args[0]
  2.1 0.0 copy-done.1
  2.1 0.0 copy-done
  2.1 3.5 %fields_first.1 = (f32[16,8,64,128]{3,2,1,0:T(8,128)S(1)}, f32[8,128]{1,0:T(8,128)S(1)}, bf16[512,2304]{1,0:T(8,128)(2,1)S(1)}, f32[8,384]{1,0:T(8,128)S(1)}, f32[8,384]{1,0:T(8,128)S(1)}) custom-call(s32[4]{0:T(128)S(1)} %copy-done.1, s32[3,8]{1,0:T(4,128)S(1)} %bitcast.9, bf16[6,256,384]{2,1,0:T(8,128)(2,1)S(1)} %bitcast.7), custom_call_target="tpu_custom_call" | custom-call | tf_op jit(solution)/shard_map/fields_first/pallas_call | solution.py:109
  5.7 4.4 %collective-permute-start = (f32[520,128]{1,0:T(8,128)S(1)}, f32[520,128]{1,0:T(8,128)S(1)}, u32[]{:S(2)}, u32[]{:S(2)}) collective-permute-start(f32[520,128]{1,0:T(8,128)S(1)} %get-tuple-element.46), channel_id=1, source_target_pairs={{0,1},{1,2},{2,3},{3,4},{4,5},{5,6},{6,7},{7,8},{8,9},{9,10},{10,1... | collective-permute-start | bytes 798728 | tf_op jit(solution)/shard_map/ppermute | solution.py:223
  10.1 9.5 %collective-permute-start.1 = (f32[520,128]{1,0:T(8,128)S(1)}, f32[520,128]{1,0:T(8,128)S(1)}, u32[]{:S(2)}, u32[]{:S(2)}) collective-permute-start(f32[520,128]{1,0:T(8,128)S(1)} %get-tuple-element.48), channel_id=1, source_target_pairs={{0,15},{1,0},{2,1},{3,2},{4,3},{5,4},{6,5},{7,6},{8,7},{9,8},{10,9... | collective-permute-start | bytes 798728 | tf_op jit(solution)/shard_map/ppermute | solution.py:226
  19.6 3.2 %fields_second.1.refs_1_ = f32[16,8,64,128]{3,2,1,0:T(8,128)S(1)} custom-call(s32[4]{0:T(128)S(1)} %copy-done.1, bf16[6,256,384]{2,1,0:T(8,128)(2,1)S(1)} %bitcast.8, f32[8,384]{1,0:T(8,128)S(1)} %get-tuple-element.40.refs_2_, f32[8,384]{1,0:T(8,128)S(1)} %get-tuple-element.41.refs_3_, ...), custom_call_target="tpu_custom_call", output_to_operand_aliasing={{}: (5, {})} | custom-call | tf_op jit(solution)/shard_map/fields_second/pallas_call | solution.py:128
  22.8 0.9 collective-permute-done.refs_3_
  23.8 1.9 %collective-permute-start.2 = (f32[520,128]{1,0:T(8,128)S(1)}, f32[520,128]{1,0:T(8,128)S(1)}, u32[]{:S(2)}, u32[]{:S(2)}) collective-permute-start(f32[520,128]{1,0:T(8,128)S(1)} %get-tuple-element.50), channel_id=1, source_target_pairs={{0,1},{1,2},{2,3},{3,4},{4,5},{5,6},{6,7},{7,8},{8,9},{9,10},{10,1... | collective-permute-start | bytes 798728 | tf_op jit(solution)/shard_map/ppermute | solution.py:223
  25.7 0.0 collective-permute-done.1.refs_3_
  25.7 4.6 %collective-permute-start.3 = (f32[520,128]{1,0:T(8,128)S(1)}, f32[520,128]{1,0:T(8,128)S(1)}, u32[]{:S(2)}, u32[]{:S(2)}) collective-permute-start(f32[520,128]{1,0:T(8,128)S(1)} %get-tuple-element.52), channel_id=1, source_target_pairs={{0,15},{1,0},{2,1},{3,2},{4,3},{5,4},{6,5},{7,6},{8,7},{9,8},{10,9... | collective-permute-start | bytes 798728 | tf_op jit(solution)/shard_map/ppermute | solution.py:226
  30.3 3.2 %collective-permute-done.2.refs_3_ = f32[520,128]{1,0:T(8,128)S(1)} collective-permute-done((f32[520,128]{1,0:T(8,128)S(1)}, f32[520,128]{1,0:T(8,128)S(1)}, u32[]{:S(2)}, u32[]{:S(2)}) %collective-permute-start.2) | collective-permute-done | bytes 266272 | tf_op jit(solution)/shard_map/ppermute | solution.py:223
  33.5 1.9 %collective-permute-start.4 = (f32[520,128]{1,0:T(8,128)S(1)}, f32[520,128]{1,0:T(8,128)S(1)}, u32[]{:S(2)}, u32[]{:S(2)}) collective-permute-start(f32[520,128]{1,0:T(8,128)S(1)} %get-tuple-element.54), channel_id=1, source_target_pairs={{0,1},{1,2},{2,3},{3,4},{4,5},{5,6},{6,7},{7,8},{8,9},{9,10},{10,1... | collective-permute-start | bytes 798728 | tf_op jit(solution)/shard_map/ppermute | solution.py:223
  35.5 0.0 collective-permute-done.3.refs_3_
  35.5 4.6 %collective-permute-start.5 = (f32[520,128]{1,0:T(8,128)S(1)}, f32[520,128]{1,0:T(8,128)S(1)}, u32[]{:S(2)}, u32[]{:S(2)}) collective-permute-start(f32[520,128]{1,0:T(8,128)S(1)} %get-tuple-element.56), channel_id=1, source_target_pairs={{0,15},{1,0},{2,1},{3,2},{4,3},{5,4},{6,5},{7,6},{8,7},{9,8},{10,9... | collective-permute-start | bytes 798728 | tf_op jit(solution)/shard_map/ppermute | solution.py:226
  40.1 2.3 %collective-permute-done.4.refs_3_ = f32[520,128]{1,0:T(8,128)S(1)} collective-permute-done((f32[520,128]{1,0:T(8,128)S(1)}, f32[520,128]{1,0:T(8,128)S(1)}, u32[]{:S(2)}, u32[]{:S(2)}) %collective-permute-start.4) | collective-permute-done | bytes 266272 | tf_op jit(solution)/shard_map/ppermute | solution.py:223
  42.4 1.9 %collective-permute-start.6 = (f32[520,128]{1,0:T(8,128)S(1)}, f32[520,128]{1,0:T(8,128)S(1)}, u32[]{:S(2)}, u32[]{:S(2)}) collective-permute-start(f32[520,128]{1,0:T(8,128)S(1)} %get-tuple-element.58), channel_id=1, source_target_pairs={{0,1},{1,2},{2,3},{3,4},{4,5},{5,6},{6,7},{7,8},{8,9},{9,10},{10,1... | collective-permute-start | bytes 798728 | tf_op jit(solution)/shard_map/ppermute | solution.py:223
  44.4 0.0 collective-permute-done.5.refs_3_
  44.4 4.6 %collective-permute-start.7 = (f32[520,128]{1,0:T(8,128)S(1)}, f32[520,128]{1,0:T(8,128)S(1)}, u32[]{:S(2)}, u32[]{:S(2)}) collective-permute-start(f32[520,128]{1,0:T(8,128)S(1)} %get-tuple-element.60), channel_id=1, source_target_pairs={{0,15},{1,0},{2,1},{3,2},{4,3},{5,4},{6,5},{7,6},{8,7},{9,8},{10,9... | collective-permute-start | bytes 798728 | tf_op jit(solution)/shard_map/ppermute | solution.py:226
  49.0 1.8 %collective-permute-done.6.refs_3_ = f32[520,128]{1,0:T(8,128)S(1)} collective-permute-done((f32[520,128]{1,0:T(8,128)S(1)}, f32[520,128]{1,0:T(8,128)S(1)}, u32[]{:S(2)}, u32[]{:S(2)}) %collective-permute-start.6) | collective-permute-done | bytes 266272 | tf_op jit(solution)/shard_map/ppermute | solution.py:223
  50.8 1.9 %collective-permute-start.8 = (f32[520,128]{1,0:T(8,128)S(1)}, f32[520,128]{1,0:T(8,128)S(1)}, u32[]{:S(2)}, u32[]{:S(2)}) collective-permute-start(f32[520,128]{1,0:T(8,128)S(1)} %get-tuple-element.62), channel_id=1, source_target_pairs={{0,1},{1,2},{2,3},{3,4},{4,5},{5,6},{6,7},{7,8},{8,9},{9,10},{10,1... | collective-permute-start | bytes 798728 | tf_op jit(solution)/shard_map/ppermute | solution.py:223
  52.8 0.0 collective-permute-done.7.refs_3_
  52.8 4.6 %collective-permute-start.9 = (f32[520,128]{1,0:T(8,128)S(1)}, f32[520,128]{1,0:T(8,128)S(1)}, u32[]{:S(2)}, u32[]{:S(2)}) collective-permute-start(f32[520,128]{1,0:T(8,128)S(1)} %get-tuple-element.64), channel_id=1, source_target_pairs={{0,15},{1,0},{2,1},{3,2},{4,3},{5,4},{6,5},{7,6},{8,7},{9,8},{10,9... | collective-permute-start | bytes 798728 | tf_op jit(solution)/shard_map/ppermute | solution.py:226
  57.4 1.8 %collective-permute-done.8.refs_3_ = f32[520,128]{1,0:T(8,128)S(1)} collective-permute-done((f32[520,128]{1,0:T(8,128)S(1)}, f32[520,128]{1,0:T(8,128)S(1)}, u32[]{:S(2)}, u32[]{:S(2)}) %collective-permute-start.8) | collective-permute-done | bytes 266272 | tf_op jit(solution)/shard_map/ppermute | solution.py:223
  59.2 1.9 %collective-permute-start.10 = (f32[520,128]{1,0:T(8,128)S(1)}, f32[520,128]{1,0:T(8,128)S(1)}, u32[]{:S(2)}, u32[]{:S(2)}) collective-permute-start(f32[520,128]{1,0:T(8,128)S(1)} %get-tuple-element.66), channel_id=1, source_target_pairs={{0,1},{1,2},{2,3},{3,4},{4,5},{5,6},{6,7},{7,8},{8,9},{9,10},{10,1... | collective-permute-start | bytes 798728 | tf_op jit(solution)/shard_map/ppermute | solution.py:223
  61.2 0.0 collective-permute-done.9.refs_3_
  61.2 4.6 %collective-permute-start.11 = (f32[520,128]{1,0:T(8,128)S(1)}, f32[520,128]{1,0:T(8,128)S(1)}, u32[]{:S(2)}, u32[]{:S(2)}) collective-permute-start(f32[520,128]{1,0:T(8,128)S(1)} %get-tuple-element.68), channel_id=1, source_target_pairs={{0,15},{1,0},{2,1},{3,2},{4,3},{5,4},{6,5},{7,6},{8,7},{9,8},{10,9... | collective-permute-start | bytes 798728 | tf_op jit(solution)/shard_map/ppermute | solution.py:226
  65.8 1.8 %collective-permute-done.10.refs_3_ = f32[520,128]{1,0:T(8,128)S(1)} collective-permute-done((f32[520,128]{1,0:T(8,128)S(1)}, f32[520,128]{1,0:T(8,128)S(1)}, u32[]{:S(2)}, u32[]{:S(2)}) %collective-permute-start.10) | collective-permute-done | bytes 266272 | tf_op jit(solution)/shard_map/ppermute | solution.py:223
  67.6 1.9 %collective-permute-start.12 = (f32[520,128]{1,0:T(8,128)S(1)}, f32[520,128]{1,0:T(8,128)S(1)}, u32[]{:S(2)}, u32[]{:S(2)}) collective-permute-start(f32[520,128]{1,0:T(8,128)S(1)} %get-tuple-element.70), channel_id=1, source_target_pairs={{0,1},{1,2},{2,3},{3,4},{4,5},{5,6},{6,7},{7,8},{8,9},{9,10},{10,1... | collective-permute-start | bytes 798728 | tf_op jit(solution)/shard_map/ppermute | solution.py:223
  69.6 0.0 collective-permute-done.11.refs_3_
  69.6 4.6 %collective-permute-start.14 = (f32[520,128]{1,0:T(8,128)S(1)}, f32[520,128]{1,0:T(8,128)S(1)}, u32[]{:S(2)}, u32[]{:S(2)}) collective-permute-start(f32[520,128]{1,0:T(8,128)S(1)} %get-tuple-element.73), channel_id=1, source_target_pairs={{0,15},{1,0},{2,1},{3,2},{4,3},{5,4},{6,5},{7,6},{8,7},{9,8},{10,9... | collective-permute-start | bytes 798728 | tf_op jit(solution)/shard_map/ppermute | solution.py:226
  74.2 2.1 %collective-permute-done.12.refs_3_ = f32[520,128]{1,0:T(8,128)S(1)} collective-permute-done((f32[520,128]{1,0:T(8,128)S(1)}, f32[520,128]{1,0:T(8,128)S(1)}, u32[]{:S(2)}, u32[]{:S(2)}) %collective-permute-start.12) | collective-permute-done | bytes 266272 | tf_op jit(solution)/shard_map/ppermute | solution.py:223
  76.3 1.9 %collective-permute-start.13 = (f32[520,128]{1,0:T(8,128)S(1)}, f32[520,128]{1,0:T(8,128)S(1)}, u32[]{:S(2)}, u32[]{:S(2)}) collective-permute-start(f32[520,128]{1,0:T(8,128)S(1)} %get-tuple-element.72), channel_id=1, source_target_pairs={{0,1},{1,2},{2,3},{3,4},{4,5},{5,6},{6,7},{7,8},{8,9},{9,10},{10,1... | collective-permute-start | bytes 798728 | tf_op jit(solution)/shard_map/ppermute | solution.py:223
  78.3 0.0 collective-permute-done.14.refs_4_
  78.3 7.8 %collective-permute-done.13.refs_3_ = f32[520,128]{1,0:T(8,128)S(1)} collective-permute-done((f32[520,128]{1,0:T(8,128)S(1)}, f32[520,128]{1,0:T(8,128)S(1)}, u32[]{:S(2)}, u32[]{:S(2)}) %collective-permute-start.13) | collective-permute-done | bytes 266272 | tf_op jit(solution)/shard_map/ppermute | solution.py:223
  86.1 0.8 final.1
  86.9 24.4 %all_to_all.5 = f32[32,16,128]{2,1,0:T(8,128)S(1)} all-to-all(f32[32,16,128]{2,1,0:T(8,128)S(1)} %get-tuple-element.74), channel_id=1, replica_groups=mesh['ta'=32,'sa'=16] {'ta'}, dimensions={0} | all-to-all | bytes 524288 | tf_op jit(solution)/shard_map/all_to_all | solution.py:238
  111.3 0.8 copy.22
  (16 shorter events, 0.5 us)
Async XLA Ops:
  0.6 1.5 %copy-start.1 = (s32[4]{0:T(128)S(1)}, s32[4]{0:T(128)}, u32[]{:S(2)}) copy-start(s32[4]{0:T(128)} %refs_0_.3) | copy-start | bytes 52
  0.6 1.5 %copy-start = (s32[8,3]{0,1:T(4,128)S(1)}, s32[8,3]{0,1:T(4,128)}, u32[]{:S(2)}) copy-start(s32[8,3]{0,1:T(4,128)} %param.4) | copy-start | bytes 292
  5.7 18.1 %collective-permute-start = (f32[520,128]{1,0:T(8,128)S(1)}, f32[520,128]{1,0:T(8,128)S(1)}, u32[]{:S(2)}, u32[]{:S(2)}) collective-permute-start(f32[520,128]{1,0:T(8,128)S(1)} %get-tuple-element.46), channel_id=1, source_target_pairs={{0,1},{1,2},{2,3},{3,4},{4,5},{5,6},{6,7},{7,8},{8,9},{9,10},{10,1... | collective-permute-start | bytes 798728 | tf_op jit(solution)/shard_map/ppermute | solution.py:223
  10.1 15.6 %collective-permute-start.1 = (f32[520,128]{1,0:T(8,128)S(1)}, f32[520,128]{1,0:T(8,128)S(1)}, u32[]{:S(2)}, u32[]{:S(2)}) collective-permute-start(f32[520,128]{1,0:T(8,128)S(1)} %get-tuple-element.48), channel_id=1, source_target_pairs={{0,15},{1,0},{2,1},{3,2},{4,3},{5,4},{6,5},{7,6},{8,7},{9,8},{10,9... | collective-permute-start | bytes 798728 | tf_op jit(solution)/shard_map/ppermute | solution.py:226
  23.8 9.8 %collective-permute-start.2 = (f32[520,128]{1,0:T(8,128)S(1)}, f32[520,128]{1,0:T(8,128)S(1)}, u32[]{:S(2)}, u32[]{:S(2)}) collective-permute-start(f32[520,128]{1,0:T(8,128)S(1)} %get-tuple-element.50), channel_id=1, source_target_pairs={{0,1},{1,2},{2,3},{3,4},{4,5},{5,6},{6,7},{7,8},{8,9},{9,10},{10,1... | collective-permute-start | bytes 798728 | tf_op jit(solution)/shard_map/ppermute | solution.py:223
  25.7 9.7 %collective-permute-start.3 = (f32[520,128]{1,0:T(8,128)S(1)}, f32[520,128]{1,0:T(8,128)S(1)}, u32[]{:S(2)}, u32[]{:S(2)}) collective-permute-start(f32[520,128]{1,0:T(8,128)S(1)} %get-tuple-element.52), channel_id=1, source_target_pairs={{0,15},{1,0},{2,1},{3,2},{4,3},{5,4},{6,5},{7,6},{8,7},{9,8},{10,9... | collective-permute-start | bytes 798728 | tf_op jit(solution)/shard_map/ppermute | solution.py:226
  33.5 8.8 %collective-permute-start.4 = (f32[520,128]{1,0:T(8,128)S(1)}, f32[520,128]{1,0:T(8,128)S(1)}, u32[]{:S(2)}, u32[]{:S(2)}) collective-permute-start(f32[520,128]{1,0:T(8,128)S(1)} %get-tuple-element.54), channel_id=1, source_target_pairs={{0,1},{1,2},{2,3},{3,4},{4,5},{5,6},{6,7},{7,8},{8,9},{9,10},{10,1... | collective-permute-start | bytes 798728 | tf_op jit(solution)/shard_map/ppermute | solution.py:223
  35.5 8.8 %collective-permute-start.5 = (f32[520,128]{1,0:T(8,128)S(1)}, f32[520,128]{1,0:T(8,128)S(1)}, u32[]{:S(2)}, u32[]{:S(2)}) collective-permute-start(f32[520,128]{1,0:T(8,128)S(1)} %get-tuple-element.56), channel_id=1, source_target_pairs={{0,15},{1,0},{2,1},{3,2},{4,3},{5,4},{6,5},{7,6},{8,7},{9,8},{10,9... | collective-permute-start | bytes 798728 | tf_op jit(solution)/shard_map/ppermute | solution.py:226
  42.4 8.4 %collective-permute-start.6 = (f32[520,128]{1,0:T(8,128)S(1)}, f32[520,128]{1,0:T(8,128)S(1)}, u32[]{:S(2)}, u32[]{:S(2)}) collective-permute-start(f32[520,128]{1,0:T(8,128)S(1)} %get-tuple-element.58), channel_id=1, source_target_pairs={{0,1},{1,2},{2,3},{3,4},{4,5},{5,6},{6,7},{7,8},{8,9},{9,10},{10,1... | collective-permute-start | bytes 798728 | tf_op jit(solution)/shard_map/ppermute | solution.py:223
  44.4 8.4 %collective-permute-start.7 = (f32[520,128]{1,0:T(8,128)S(1)}, f32[520,128]{1,0:T(8,128)S(1)}, u32[]{:S(2)}, u32[]{:S(2)}) collective-permute-start(f32[520,128]{1,0:T(8,128)S(1)} %get-tuple-element.60), channel_id=1, source_target_pairs={{0,15},{1,0},{2,1},{3,2},{4,3},{5,4},{6,5},{7,6},{8,7},{9,8},{10,9... | collective-permute-start | bytes 798728 | tf_op jit(solution)/shard_map/ppermute | solution.py:226
  50.8 8.4 %collective-permute-start.8 = (f32[520,128]{1,0:T(8,128)S(1)}, f32[520,128]{1,0:T(8,128)S(1)}, u32[]{:S(2)}, u32[]{:S(2)}) collective-permute-start(f32[520,128]{1,0:T(8,128)S(1)} %get-tuple-element.62), channel_id=1, source_target_pairs={{0,1},{1,2},{2,3},{3,4},{4,5},{5,6},{6,7},{7,8},{8,9},{9,10},{10,1... | collective-permute-start | bytes 798728 | tf_op jit(solution)/shard_map/ppermute | solution.py:223
  52.8 8.4 %collective-permute-start.9 = (f32[520,128]{1,0:T(8,128)S(1)}, f32[520,128]{1,0:T(8,128)S(1)}, u32[]{:S(2)}, u32[]{:S(2)}) collective-permute-start(f32[520,128]{1,0:T(8,128)S(1)} %get-tuple-element.64), channel_id=1, source_target_pairs={{0,15},{1,0},{2,1},{3,2},{4,3},{5,4},{6,5},{7,6},{8,7},{9,8},{10,9... | collective-permute-start | bytes 798728 | tf_op jit(solution)/shard_map/ppermute | solution.py:226
  59.2 8.4 %collective-permute-start.10 = (f32[520,128]{1,0:T(8,128)S(1)}, f32[520,128]{1,0:T(8,128)S(1)}, u32[]{:S(2)}, u32[]{:S(2)}) collective-permute-start(f32[520,128]{1,0:T(8,128)S(1)} %get-tuple-element.66), channel_id=1, source_target_pairs={{0,1},{1,2},{2,3},{3,4},{4,5},{5,6},{6,7},{7,8},{8,9},{9,10},{10,1... | collective-permute-start | bytes 798728 | tf_op jit(solution)/shard_map/ppermute | solution.py:223
  61.2 8.4 %collective-permute-start.11 = (f32[520,128]{1,0:T(8,128)S(1)}, f32[520,128]{1,0:T(8,128)S(1)}, u32[]{:S(2)}, u32[]{:S(2)}) collective-permute-start(f32[520,128]{1,0:T(8,128)S(1)} %get-tuple-element.68), channel_id=1, source_target_pairs={{0,15},{1,0},{2,1},{3,2},{4,3},{5,4},{6,5},{7,6},{8,7},{9,8},{10,9... | collective-permute-start | bytes 798728 | tf_op jit(solution)/shard_map/ppermute | solution.py:226
  67.6 8.7 %collective-permute-start.12 = (f32[520,128]{1,0:T(8,128)S(1)}, f32[520,128]{1,0:T(8,128)S(1)}, u32[]{:S(2)}, u32[]{:S(2)}) collective-permute-start(f32[520,128]{1,0:T(8,128)S(1)} %get-tuple-element.70), channel_id=1, source_target_pairs={{0,1},{1,2},{2,3},{3,4},{4,5},{5,6},{6,7},{7,8},{8,9},{9,10},{10,1... | collective-permute-start | bytes 798728 | tf_op jit(solution)/shard_map/ppermute | solution.py:223
  69.6 8.6 %collective-permute-start.14 = (f32[520,128]{1,0:T(8,128)S(1)}, f32[520,128]{1,0:T(8,128)S(1)}, u32[]{:S(2)}, u32[]{:S(2)}) collective-permute-start(f32[520,128]{1,0:T(8,128)S(1)} %get-tuple-element.73), channel_id=1, source_target_pairs={{0,15},{1,0},{2,1},{3,2},{4,3},{5,4},{6,5},{7,6},{8,7},{9,8},{10,9... | collective-permute-start | bytes 798728 | tf_op jit(solution)/shard_map/ppermute | solution.py:226
  76.3 9.7 %collective-permute-start.13 = (f32[520,128]{1,0:T(8,128)S(1)}, f32[520,128]{1,0:T(8,128)S(1)}, u32[]{:S(2)}, u32[]{:S(2)}) collective-permute-start(f32[520,128]{1,0:T(8,128)S(1)} %get-tuple-element.72), channel_id=1, source_target_pairs={{0,1},{1,2},{2,3},{3,4},{4,5},{5,6},{6,7},{7,8},{8,9},{9,10},{10,1... | collective-permute-start | bytes 798728 | tf_op jit(solution)/shard_map/ppermute | solution.py:223

commit v5 on v4

--- a/solution.py
+++ b/solution.py
@@ -37,26 +37,27 @@
             left_ref[pl.ds((2 * k + 1) * BS, BS), after] = re
 
 
-def fill_right(n, b, count, order_ref, x_ref, cosines, sines, right_ref):
-    planes = x_ref.shape[-1]
+def fill_right(n, b, left_ref, cosines, sines, right_ref):
+    count, planes = cosines.shape
     half = NC * planes
-    stored = pl.ds(pl.multiple_of(order_ref[b] * BS, BS), BS)
+    held = pl.ds(pl.multiple_of(b * 2 * BS, 2 * BS), BS)
     for c in range(NC):
-        re = x_ref[c, stored, :].astype(jnp.float32)
-        im = x_ref[NC + c, stored, :].astype(jnp.float32)
+        lanes, after = pl.ds(c * planes, planes), pl.ds(half + c * planes, planes)
+        re = left_ref[held, lanes].astype(jnp.float32)
+        im = left_ref[held, after].astype(jnp.float32)
         for p in range(count):
             cos = cosines[p : p + 1]
             sin = sines[p : p + 1]
             rows = pl.ds((n * count + p) * BS, BS)
-            right_ref[rows, pl.ds(c * planes, planes)] = (re * cos + im * sin).astype(jnp.bfloat16)
-            right_ref[rows, pl.ds(half + c * planes, planes)] = (im * cos - re * sin).astype(jnp.bfloat16)
-
-
-def multiply(columns, scale, order_ref, x_ref, cosines, sines, right_ref, left_ref, out_ref):
+            right_ref[rows, lanes] = (re * cos + im * sin).astype(jnp.bfloat16)
+            right_ref[rows, after] = (im * cos - re * sin).astype(jnp.bfloat16)
+
+
+def multiply(columns, scale, cosines, sines, right_ref, left_ref, out_ref):
     count = cosines.shape[0]
     size = count * BS
     for n, b in enumerate(columns):
-        fill_right(n, b, count, order_ref, x_ref, cosines, sines, right_ref)
+        fill_right(n, b, left_ref, cosines, sines, right_ref)
     product = lax.dot_general(
         right_ref[...], left_ref[...], (((1,), (1,)), ((), ())), preferred_element_type=jnp.float32
     )
@@ -86,7 +87,7 @@
     cos_ref[...] = cosines
     sin_ref[...] = sines
     fill_left(order_ref, x_ref, left_ref)
-    multiply(near_columns()[0], scale, order_ref, x_ref, cosines, sines, right_ref, left_ref, out_ref)
+    multiply(near_columns()[0], scale, cosines, sines, right_ref, left_ref, out_ref)
     squares = jnp.zeros((NV, 128), jnp.float32)
     for k in range(PARTS):
         for l in range(planes // 128):
@@ -99,7 +100,7 @@
 
 
 def second_kernel(scale, order_ref, x_ref, cos_ref, sin_ref, left_ref, made_ref, after_ref, out_ref, right_ref):
-    multiply(near_columns()[1], scale, order_ref, x_ref, cos_ref[...], sin_ref[...], right_ref, left_ref, out_ref)
+    multiply(near_columns()[1], scale, cos_ref[...], sin_ref[...], right_ref, left_ref, out_ref)
 
 
 def first_half(parts, momenta, block_order, scale):

time: 113 us -> 113 us (level)
  no operation moved by 1% of the time
where the time goes in v5:
time: 113 us; the launch traced here: 112 us
  starting transfers between devices  54.8 us (48%)
  blocking collectives  24.5 us (22%)
  waiting for transfers between devices  21.7 us (19%)
  Pallas kernels  8.1 us (7%)
  local copies, waits for them, and re-layouts  2.23 us (2%)
    ppermute x7, starting transfers between devices, body(): l = lax.ppermute(send, 'sa', down)  37 us
    all_to_all x1, blocking collectives, body(): tiles = lax.all_to_all(tiles, 'ta', 0, 0, tiled=True)  24.5 us
    ppermute x8, waiting for transfers between devices, body(): r = lax.ppermute(send, 'sa', up)  21.6 us
    ppermute x8, starting transfers between devices, body(): r = lax.ppermute(send, 'sa', up)  17.8 us
    pallas_call x1, Pallas kernels, first_half(): pl.pallas_call(lambda *refs: first_kernel(scale, *refs), in_specs=[pl.Blo...  3.54 us
    pallas_call x1, Pallas kernels, second_half(): pl.pallas_call(lambda *refs: second_kernel(scale, *refs), in_specs=[pl.Bl...  3.24 us
  transfers between devices with their start and end apart: 15, of which 8 were waited for; matrix products, arithmetic and copies ran while one was open for 0% of the time, Pallas kernels for 3%

profile of v5, /device:TPU:1, one launch (start us, length us, event | category | flops | bytes accessed | tf_op | source)
XLA Modules:
  0.0 112.1 jit_solution(14771708958148667067)
XLA Ops:
  0.6 0.0 copy-start.1
  0.6 0.0 copy-start
  0.6 1.4 %copy.21 = bf16[1,256,2,3,1,384]{5,1,3,2,4,0:T(8,128)(2,1)S(1)} copy(bf16[1,256,2,3,1,384]{5,2,4,3,1,0:T(2,128)(2,1)} %param.3) | data formatting | bytes 2359296 | tf_op args[0]
  2.1 0.0 copy-done.1
  2.1 0.0 copy-done
  2.1 3.5 %fields_first.1 = (f32[16,8,64,128]{3,2,1,0:T(8,128)S(1)}, f32[8,128]{1,0:T(8,128)S(1)}, bf16[512,2304]{1,0:T(8,128)(2,1)S(1)}, f32[8,384]{1,0:T(8,128)S(1)}, f32[8,384]{1,0:T(8,128)S(1)}) custom-call(s32[4]{0:T(128)S(1)} %copy-done.1, s32[3,8]{1,0:T(4,128)S(1)} %bitcast.9, bf16[6,256,384]{2,1,0:T(8,128)(2,1)S(1)} %bitcast.7), custom_call_target="tpu_custom_call" | custom-call | tf_op jit(solution)/shard_map/fields_first/pallas_call | solution.py:110
  5.7 4.4 %collective-permute-start = (f32[520,128]{1,0:T(8,128)S(1)}, f32[520,128]{1,0:T(8,128)S(1)}, u32[]{:S(2)}, u32[]{:S(2)}) collective-permute-start(f32[520,128]{1,0:T(8,128)S(1)} %get-tuple-element.46), channel_id=1, source_target_pairs={{0,1},{1,2},{2,3},{3,4},{4,5},{5,6},{6,7},{7,8},{8,9},{9,10},{10,1... | collective-permute-start | bytes 798728 | tf_op jit(solution)/shard_map/ppermute | solution.py:224
  10.1 9.5 %collective-permute-start.1 = (f32[520,128]{1,0:T(8,128)S(1)}, f32[520,128]{1,0:T(8,128)S(1)}, u32[]{:S(2)}, u32[]{:S(2)}) collective-permute-start(f32[520,128]{1,0:T(8,128)S(1)} %get-tuple-element.48), channel_id=1, source_target_pairs={{0,15},{1,0},{2,1},{3,2},{4,3},{5,4},{6,5},{7,6},{8,7},{9,8},{10,9... | collective-permute-start | bytes 798728 | tf_op jit(solution)/shard_map/ppermute | solution.py:227
  19.6 3.2 %fields_second.1.refs_1_ = f32[16,8,64,128]{3,2,1,0:T(8,128)S(1)} custom-call(s32[4]{0:T(128)S(1)} %copy-done.1, bf16[6,256,384]{2,1,0:T(8,128)(2,1)S(1)} %bitcast.8, f32[8,384]{1,0:T(8,128)S(1)} %get-tuple-element.40.refs_2_, f32[8,384]{1,0:T(8,128)S(1)} %get-tuple-element.41.refs_3_, ...), custom_call_target="tpu_custom_call", output_to_operand_aliasing={{}: (5, {})} | custom-call | tf_op jit(solution)/shard_map/fields_second/pallas_call | solution.py:129
  22.9 0.9 collective-permute-done.refs_3_
  23.8 1.9 %collective-permute-start.2 = (f32[520,128]{1,0:T(8,128)S(1)}, f32[520,128]{1,0:T(8,128)S(1)}, u32[]{:S(2)}, u32[]{:S(2)}) collective-permute-start(f32[520,128]{1,0:T(8,128)S(1)} %get-tuple-element.50), channel_id=1, source_target_pairs={{0,1},{1,2},{2,3},{3,4},{4,5},{5,6},{6,7},{7,8},{8,9},{9,10},{10,1... | collective-permute-start | bytes 798728 | tf_op jit(solution)/shard_map/ppermute | solution.py:224
  25.7 0.0 collective-permute-done.1.refs_3_
  25.8 4.6 %collective-permute-start.3 = (f32[520,128]{1,0:T(8,128)S(1)}, f32[520,128]{1,0:T(8,128)S(1)}, u32[]{:S(2)}, u32[]{:S(2)}) collective-permute-start(f32[520,128]{1,0:T(8,128)S(1)} %get-tuple-element.52), channel_id=1, source_target_pairs={{0,15},{1,0},{2,1},{3,2},{4,3},{5,4},{6,5},{7,6},{8,7},{9,8},{10,9... | collective-permute-start | bytes 798728 | tf_op jit(solution)/shard_map/ppermute | solution.py:227
  30.4 3.2 %collective-permute-done.2.refs_3_ = f32[520,128]{1,0:T(8,128)S(1)} collective-permute-done((f32[520,128]{1,0:T(8,128)S(1)}, f32[520,128]{1,0:T(8,128)S(1)}, u32[]{:S(2)}, u32[]{:S(2)}) %collective-permute-start.2) | collective-permute-done | bytes 266272 | tf_op jit(solution)/shard_map/ppermute | solution.py:224
  33.6 1.9 %collective-permute-start.4 = (f32[520,128]{1,0:T(8,128)S(1)}, f32[520,128]{1,0:T(8,128)S(1)}, u32[]{:S(2)}, u32[]{:S(2)}) collective-permute-start(f32[520,128]{1,0:T(8,128)S(1)} %get-tuple-element.54), channel_id=1, source_target_pairs={{0,1},{1,2},{2,3},{3,4},{4,5},{5,6},{6,7},{7,8},{8,9},{9,10},{10,1... | collective-permute-start | bytes 798728 | tf_op jit(solution)/shard_map/ppermute | solution.py:224
  35.5 0.0 collective-permute-done.3.refs_3_
  35.6 4.6 %collective-permute-start.5 = (f32[520,128]{1,0:T(8,128)S(1)}, f32[520,128]{1,0:T(8,128)S(1)}, u32[]{:S(2)}, u32[]{:S(2)}) collective-permute-start(f32[520,128]{1,0:T(8,128)S(1)} %get-tuple-element.56), channel_id=1, source_target_pairs={{0,15},{1,0},{2,1},{3,2},{4,3},{5,4},{6,5},{7,6},{8,7},{9,8},{10,9... | collective-permute-start | bytes 798728 | tf_op jit(solution)/shard_map/ppermute | solution.py:227
  40.2 2.3 %collective-permute-done.4.refs_3_ = f32[520,128]{1,0:T(8,128)S(1)} collective-permute-done((f32[520,128]{1,0:T(8,128)S(1)}, f32[520,128]{1,0:T(8,128)S(1)}, u32[]{:S(2)}, u32[]{:S(2)}) %collective-permute-start.4) | collective-permute-done | bytes 266272 | tf_op jit(solution)/shard_map/ppermute | solution.py:224
  42.5 1.9 %collective-permute-start.6 = (f32[520,128]{1,0:T(8,128)S(1)}, f32[520,128]{1,0:T(8,128)S(1)}, u32[]{:S(2)}, u32[]{:S(2)}) collective-permute-start(f32[520,128]{1,0:T(8,128)S(1)} %get-tuple-element.58), channel_id=1, source_target_pairs={{0,1},{1,2},{2,3},{3,4},{4,5},{5,6},{6,7},{7,8},{8,9},{9,10},{10,1... | collective-permute-start | bytes 798728 | tf_op jit(solution)/shard_map/ppermute | solution.py:224
  44.4 0.0 collective-permute-done.5.refs_3_
  44.5 4.6 %collective-permute-start.7 = (f32[520,128]{1,0:T(8,128)S(1)}, f32[520,128]{1,0:T(8,128)S(1)}, u32[]{:S(2)}, u32[]{:S(2)}) collective-permute-start(f32[520,128]{1,0:T(8,128)S(1)} %get-tuple-element.60), channel_id=1, source_target_pairs={{0,15},{1,0},{2,1},{3,2},{4,3},{5,4},{6,5},{7,6},{8,7},{9,8},{10,9... | collective-permute-start | bytes 798728 | tf_op jit(solution)/shard_map/ppermute | solution.py:227
  49.0 1.8 %collective-permute-done.6.refs_3_ = f32[520,128]{1,0:T(8,128)S(1)} collective-permute-done((f32[520,128]{1,0:T(8,128)S(1)}, f32[520,128]{1,0:T(8,128)S(1)}, u32[]{:S(2)}, u32[]{:S(2)}) %collective-permute-start.6) | collective-permute-done | bytes 266272 | tf_op jit(solution)/shard_map/ppermute | solution.py:224
  50.9 1.9 %collective-permute-start.8 = (f32[520,128]{1,0:T(8,128)S(1)}, f32[520,128]{1,0:T(8,128)S(1)}, u32[]{:S(2)}, u32[]{:S(2)}) collective-permute-start(f32[520,128]{1,0:T(8,128)S(1)} %get-tuple-element.62), channel_id=1, source_target_pairs={{0,1},{1,2},{2,3},{3,4},{4,5},{5,6},{6,7},{7,8},{8,9},{9,10},{10,1... | collective-permute-start | bytes 798728 | tf_op jit(solution)/shard_map/ppermute | solution.py:224
  52.8 0.0 collective-permute-done.7.refs_3_
  52.9 4.6 %collective-permute-start.9 = (f32[520,128]{1,0:T(8,128)S(1)}, f32[520,128]{1,0:T(8,128)S(1)}, u32[]{:S(2)}, u32[]{:S(2)}) collective-permute-start(f32[520,128]{1,0:T(8,128)S(1)} %get-tuple-element.64), channel_id=1, source_target_pairs={{0,15},{1,0},{2,1},{3,2},{4,3},{5,4},{6,5},{7,6},{8,7},{9,8},{10,9... | collective-permute-start | bytes 798728 | tf_op jit(solution)/shard_map/ppermute | solution.py:227
  57.4 1.8 %collective-permute-done.8.refs_3_ = f32[520,128]{1,0:T(8,128)S(1)} collective-permute-done((f32[520,128]{1,0:T(8,128)S(1)}, f32[520,128]{1,0:T(8,128)S(1)}, u32[]{:S(2)}, u32[]{:S(2)}) %collective-permute-start.8) | collective-permute-done | bytes 266272 | tf_op jit(solution)/shard_map/ppermute | solution.py:224
  59.3 1.9 %collective-permute-start.10 = (f32[520,128]{1,0:T(8,128)S(1)}, f32[520,128]{1,0:T(8,128)S(1)}, u32[]{:S(2)}, u32[]{:S(2)}) collective-permute-start(f32[520,128]{1,0:T(8,128)S(1)} %get-tuple-element.66), channel_id=1, source_target_pairs={{0,1},{1,2},{2,3},{3,4},{4,5},{5,6},{6,7},{7,8},{8,9},{9,10},{10,1... | collective-permute-start | bytes 798728 | tf_op jit(solution)/shard_map/ppermute | solution.py:224
  61.2 0.0 collective-permute-done.9.refs_3_
  61.3 4.6 %collective-permute-start.11 = (f32[520,128]{1,0:T(8,128)S(1)}, f32[520,128]{1,0:T(8,128)S(1)}, u32[]{:S(2)}, u32[]{:S(2)}) collective-permute-start(f32[520,128]{1,0:T(8,128)S(1)} %get-tuple-element.68), channel_id=1, source_target_pairs={{0,15},{1,0},{2,1},{3,2},{4,3},{5,4},{6,5},{7,6},{8,7},{9,8},{10,9... | collective-permute-start | bytes 798728 | tf_op jit(solution)/shard_map/ppermute | solution.py:227
  65.9 1.8 %collective-permute-done.10.refs_3_ = f32[520,128]{1,0:T(8,128)S(1)} collective-permute-done((f32[520,128]{1,0:T(8,128)S(1)}, f32[520,128]{1,0:T(8,128)S(1)}, u32[]{:S(2)}, u32[]{:S(2)}) %collective-permute-start.10) | collective-permute-done | bytes 266272 | tf_op jit(solution)/shard_map/ppermute | solution.py:224
  67.7 1.9 %collective-permute-start.12 = (f32[520,128]{1,0:T(8,128)S(1)}, f32[520,128]{1,0:T(8,128)S(1)}, u32[]{:S(2)}, u32[]{:S(2)}) collective-permute-start(f32[520,128]{1,0:T(8,128)S(1)} %get-tuple-element.70), channel_id=1, source_target_pairs={{0,1},{1,2},{2,3},{3,4},{4,5},{5,6},{6,7},{7,8},{8,9},{9,10},{10,1... | collective-permute-start | bytes 798728 | tf_op jit(solution)/shard_map/ppermute | solution.py:224
  69.6 0.0 collective-permute-done.11.refs_3_
  69.7 4.6 %collective-permute-start.14 = (f32[520,128]{1,0:T(8,128)S(1)}, f32[520,128]{1,0:T(8,128)S(1)}, u32[]{:S(2)}, u32[]{:S(2)}) collective-permute-start(f32[520,128]{1,0:T(8,128)S(1)} %get-tuple-element.73), channel_id=1, source_target_pairs={{0,15},{1,0},{2,1},{3,2},{4,3},{5,4},{6,5},{7,6},{8,7},{9,8},{10,9... | collective-permute-start | bytes 798728 | tf_op jit(solution)/shard_map/ppermute | solution.py:227
  74.3 2.1 %collective-permute-done.12.refs_3_ = f32[520,128]{1,0:T(8,128)S(1)} collective-permute-done((f32[520,128]{1,0:T(8,128)S(1)}, f32[520,128]{1,0:T(8,128)S(1)}, u32[]{:S(2)}, u32[]{:S(2)}) %collective-permute-start.12) | collective-permute-done | bytes 266272 | tf_op jit(solution)/shard_map/ppermute | solution.py:224
  76.4 1.9 %collective-permute-start.13 = (f32[520,128]{1,0:T(8,128)S(1)}, f32[520,128]{1,0:T(8,128)S(1)}, u32[]{:S(2)}, u32[]{:S(2)}) collective-permute-start(f32[520,128]{1,0:T(8,128)S(1)} %get-tuple-element.72), channel_id=1, source_target_pairs={{0,1},{1,2},{2,3},{3,4},{4,5},{5,6},{6,7},{7,8},{8,9},{9,10},{10,1... | collective-permute-start | bytes 798728 | tf_op jit(solution)/shard_map/ppermute | solution.py:224
  78.3 0.0 collective-permute-done.14.refs_4_
  78.3 7.8 %collective-permute-done.13.refs_3_ = f32[520,128]{1,0:T(8,128)S(1)} collective-permute-done((f32[520,128]{1,0:T(8,128)S(1)}, f32[520,128]{1,0:T(8,128)S(1)}, u32[]{:S(2)}, u32[]{:S(2)}) %collective-permute-start.13) | collective-permute-done | bytes 266272 | tf_op jit(solution)/shard_map/ppermute | solution.py:224
  86.1 0.8 final.1
  86.9 24.5 %all_to_all.5 = f32[32,16,128]{2,1,0:T(8,128)S(1)} all-to-all(f32[32,16,128]{2,1,0:T(8,128)S(1)} %get-tuple-element.74), channel_id=1, replica_groups=mesh['ta'=32,'sa'=16] {'ta'}, dimensions={0} | all-to-all | bytes 524288 | tf_op jit(solution)/shard_map/all_to_all | solution.py:239
  111.4 0.8 copy.22
  (16 shorter events, 0.5 us)
Async XLA Ops:
  0.6 1.5 %copy-start.1 = (s32[4]{0:T(128)S(1)}, s32[4]{0:T(128)}, u32[]{:S(2)}) copy-start(s32[4]{0:T(128)} %refs_0_.3) | copy-start | bytes 52
  0.6 1.5 %copy-start = (s32[8,3]{0,1:T(4,128)S(1)}, s32[8,3]{0,1:T(4,128)}, u32[]{:S(2)}) copy-start(s32[8,3]{0,1:T(4,128)} %param.4) | copy-start | bytes 292
  5.7 18.1 %collective-permute-start = (f32[520,128]{1,0:T(8,128)S(1)}, f32[520,128]{1,0:T(8,128)S(1)}, u32[]{:S(2)}, u32[]{:S(2)}) collective-permute-start(f32[520,128]{1,0:T(8,128)S(1)} %get-tuple-element.46), channel_id=1, source_target_pairs={{0,1},{1,2},{2,3},{3,4},{4,5},{5,6},{6,7},{7,8},{8,9},{9,10},{10,1... | collective-permute-start | bytes 798728 | tf_op jit(solution)/shard_map/ppermute | solution.py:224
  10.1 15.6 %collective-permute-start.1 = (f32[520,128]{1,0:T(8,128)S(1)}, f32[520,128]{1,0:T(8,128)S(1)}, u32[]{:S(2)}, u32[]{:S(2)}) collective-permute-start(f32[520,128]{1,0:T(8,128)S(1)} %get-tuple-element.48), channel_id=1, source_target_pairs={{0,15},{1,0},{2,1},{3,2},{4,3},{5,4},{6,5},{7,6},{8,7},{9,8},{10,9... | collective-permute-start | bytes 798728 | tf_op jit(solution)/shard_map/ppermute | solution.py:227
  23.8 9.8 %collective-permute-start.2 = (f32[520,128]{1,0:T(8,128)S(1)}, f32[520,128]{1,0:T(8,128)S(1)}, u32[]{:S(2)}, u32[]{:S(2)}) collective-permute-start(f32[520,128]{1,0:T(8,128)S(1)} %get-tuple-element.50), channel_id=1, source_target_pairs={{0,1},{1,2},{2,3},{3,4},{4,5},{5,6},{6,7},{7,8},{8,9},{9,10},{10,1... | collective-permute-start | bytes 798728 | tf_op jit(solution)/shard_map/ppermute | solution.py:224
  25.8 9.7 %collective-permute-start.3 = (f32[520,128]{1,0:T(8,128)S(1)}, f32[520,128]{1,0:T(8,128)S(1)}, u32[]{:S(2)}, u32[]{:S(2)}) collective-permute-start(f32[520,128]{1,0:T(8,128)S(1)} %get-tuple-element.52), channel_id=1, source_target_pairs={{0,15},{1,0},{2,1},{3,2},{4,3},{5,4},{6,5},{7,6},{8,7},{9,8},{10,9... | collective-permute-start | bytes 798728 | tf_op jit(solution)/shard_map/ppermute | solution.py:227
  33.6 8.8 %collective-permute-start.4 = (f32[520,128]{1,0:T(8,128)S(1)}, f32[520,128]{1,0:T(8,128)S(1)}, u32[]{:S(2)}, u32[]{:S(2)}) collective-permute-start(f32[520,128]{1,0:T(8,128)S(1)} %get-tuple-element.54), channel_id=1, source_target_pairs={{0,1},{1,2},{2,3},{3,4},{4,5},{5,6},{6,7},{7,8},{8,9},{9,10},{10,1... | collective-permute-start | bytes 798728 | tf_op jit(solution)/shard_map/ppermute | solution.py:224
  35.6 8.8 %collective-permute-start.5 = (f32[520,128]{1,0:T(8,128)S(1)}, f32[520,128]{1,0:T(8,128)S(1)}, u32[]{:S(2)}, u32[]{:S(2)}) collective-permute-start(f32[520,128]{1,0:T(8,128)S(1)} %get-tuple-element.56), channel_id=1, source_target_pairs={{0,15},{1,0},{2,1},{3,2},{4,3},{5,4},{6,5},{7,6},{8,7},{9,8},{10,9... | collective-permute-start | bytes 798728 | tf_op jit(solution)/shard_map/ppermute | solution.py:227
  42.5 8.4 %collective-permute-start.6 = (f32[520,128]{1,0:T(8,128)S(1)}, f32[520,128]{1,0:T(8,128)S(1)}, u32[]{:S(2)}, u32[]{:S(2)}) collective-permute-start(f32[520,128]{1,0:T(8,128)S(1)} %get-tuple-element.58), channel_id=1, source_target_pairs={{0,1},{1,2},{2,3},{3,4},{4,5},{5,6},{6,7},{7,8},{8,9},{9,10},{10,1... | collective-permute-start | bytes 798728 | tf_op jit(solution)/shard_map/ppermute | solution.py:224
  44.5 8.4 %collective-permute-start.7 = (f32[520,128]{1,0:T(8,128)S(1)}, f32[520,128]{1,0:T(8,128)S(1)}, u32[]{:S(2)}, u32[]{:S(2)}) collective-permute-start(f32[520,128]{1,0:T(8,128)S(1)} %get-tuple-element.60), channel_id=1, source_target_pairs={{0,15},{1,0},{2,1},{3,2},{4,3},{5,4},{6,5},{7,6},{8,7},{9,8},{10,9... | collective-permute-start | bytes 798728 | tf_op jit(solution)/shard_map/ppermute | solution.py:227
  50.9 8.4 %collective-permute-start.8 = (f32[520,128]{1,0:T(8,128)S(1)}, f32[520,128]{1,0:T(8,128)S(1)}, u32[]{:S(2)}, u32[]{:S(2)}) collective-permute-start(f32[520,128]{1,0:T(8,128)S(1)} %get-tuple-element.62), channel_id=1, source_target_pairs={{0,1},{1,2},{2,3},{3,4},{4,5},{5,6},{6,7},{7,8},{8,9},{9,10},{10,1... | collective-permute-start | bytes 798728 | tf_op jit(solution)/shard_map/ppermute | solution.py:224
  52.9 8.4 %collective-permute-start.9 = (f32[520,128]{1,0:T(8,128)S(1)}, f32[520,128]{1,0:T(8,128)S(1)}, u32[]{:S(2)}, u32[]{:S(2)}) collective-permute-start(f32[520,128]{1,0:T(8,128)S(1)} %get-tuple-element.64), channel_id=1, source_target_pairs={{0,15},{1,0},{2,1},{3,2},{4,3},{5,4},{6,5},{7,6},{8,7},{9,8},{10,9... | collective-permute-start | bytes 798728 | tf_op jit(solution)/shard_map/ppermute | solution.py:227
  59.3 8.4 %collective-permute-start.10 = (f32[520,128]{1,0:T(8,128)S(1)}, f32[520,128]{1,0:T(8,128)S(1)}, u32[]{:S(2)}, u32[]{:S(2)}) collective-permute-start(f32[520,128]{1,0:T(8,128)S(1)} %get-tuple-element.66), channel_id=1, source_target_pairs={{0,1},{1,2},{2,3},{3,4},{4,5},{5,6},{6,7},{7,8},{8,9},{9,10},{10,1... | collective-permute-start | bytes 798728 | tf_op jit(solution)/shard_map/ppermute | solution.py:224
  61.3 8.4 %collective-permute-start.11 = (f32[520,128]{1,0:T(8,128)S(1)}, f32[520,128]{1,0:T(8,128)S(1)}, u32[]{:S(2)}, u32[]{:S(2)}) collective-permute-start(f32[520,128]{1,0:T(8,128)S(1)} %get-tuple-element.68), channel_id=1, source_target_pairs={{0,15},{1,0},{2,1},{3,2},{4,3},{5,4},{6,5},{7,6},{8,7},{9,8},{10,9... | collective-permute-start | bytes 798728 | tf_op jit(solution)/shard_map/ppermute | solution.py:227
  67.7 8.7 %collective-permute-start.12 = (f32[520,128]{1,0:T(8,128)S(1)}, f32[520,128]{1,0:T(8,128)S(1)}, u32[]{:S(2)}, u32[]{:S(2)}) collective-permute-start(f32[520,128]{1,0:T(8,128)S(1)} %get-tuple-element.70), channel_id=1, source_target_pairs={{0,1},{1,2},{2,3},{3,4},{4,5},{5,6},{6,7},{7,8},{8,9},{9,10},{10,1... | collective-permute-start | bytes 798728 | tf_op jit(solution)/shard_map/ppermute | solution.py:224
  69.7 8.6 %collective-permute-start.14 = (f32[520,128]{1,0:T(8,128)S(1)}, f32[520,128]{1,0:T(8,128)S(1)}, u32[]{:S(2)}, u32[]{:S(2)}) collective-permute-start(f32[520,128]{1,0:T(8,128)S(1)} %get-tuple-element.73), channel_id=1, source_target_pairs={{0,15},{1,0},{2,1},{3,2},{4,3},{5,4},{6,5},{7,6},{8,7},{9,8},{10,9... | collective-permute-start | bytes 798728 | tf_op jit(solution)/shard_map/ppermute | solution.py:227
  76.4 9.7 %collective-permute-start.13 = (f32[520,128]{1,0:T(8,128)S(1)}, f32[520,128]{1,0:T(8,128)S(1)}, u32[]{:S(2)}, u32[]{:S(2)}) collective-permute-start(f32[520,128]{1,0:T(8,128)S(1)} %get-tuple-element.72), channel_id=1, source_target_pairs={{0,1},{1,2},{2,3},{3,4},{4,5},{5,6},{6,7},{7,8},{8,9},{9,10},{10,1... | collective-permute-start | bytes 798728 | tf_op jit(solution)/shard_map/ppermute | solution.py:224

commit v6 on v5

--- a/solution.py
+++ b/solution.py
@@ -19,7 +19,7 @@
 def near_columns():
     first = lax.rem(lax.axis_index("sa") + lax.axis_size("sa") // 2, NBLK)
     columns = [lax.rem(first + k, NBLK) for k in range(NBLK)]
-    return columns[:2], columns[2:]
+    return columns
 
 
 def fill_left(order_ref, x_ref, left_ref):
@@ -87,7 +87,7 @@
     cos_ref[...] = cosines
     sin_ref[...] = sines
     fill_left(order_ref, x_ref, left_ref)
-    multiply(near_columns()[0], scale, cosines, sines, right_ref, left_ref, out_ref)
+    multiply(near_columns()[:1], scale, cosines, sines, right_ref, left_ref, out_ref)
     squares = jnp.zeros((NV, 128), jnp.float32)
     for k in range(PARTS):
         for l in range(planes // 128):
@@ -99,8 +99,8 @@
         nrm_ref[pl.ds(k, 1)] = sums[:, k * 128 : (k + 1) * 128]
 
 
-def second_kernel(scale, order_ref, x_ref, cos_ref, sin_ref, left_ref, made_ref, after_ref, out_ref, right_ref):
-    multiply(near_columns()[1], scale, cos_ref[...], sin_ref[...], right_ref, left_ref, out_ref)
+def more_kernel(cut, scale, cos_ref, sin_ref, left_ref, made_ref, after_ref, out_ref, right_ref):
+    multiply(near_columns()[cut], scale, cos_ref[...], sin_ref[...], right_ref, left_ref, out_ref)
 
 
 def first_half(parts, momenta, block_order, scale):
@@ -118,24 +118,25 @@
             jax.ShapeDtypeStruct((count, planes), jnp.float32),
             jax.ShapeDtypeStruct((count, planes), jnp.float32),
         ],
-        scratch_shapes=[pltpu.VMEM((count * 2 * BS, depth), jnp.bfloat16)],
+        scratch_shapes=[pltpu.VMEM((count * BS, depth), jnp.bfloat16)],
         compiler_params=CP,
         name="fields_first",
     )(block_order, momenta.T, parts)
 
 
-def second_half(parts, block_order, made, after, scale):
-    fields, _, left, cosines, sines = made
+def more_columns(cut, made, fields, after, scale):
+    _, _, left, cosines, sines = made
+    columns = cut.stop - cut.start
     return pl.pallas_call(
-        lambda *refs: second_kernel(scale, *refs),
-        in_specs=[pl.BlockSpec(memory_space=pltpu.SMEM)] + vm(5) + [pl.BlockSpec(memory_space=pl.ANY)],
+        lambda *refs: more_kernel(cut, scale, *refs),
+        in_specs=vm(4) + [pl.BlockSpec(memory_space=pl.ANY)],
         out_specs=vm(1)[0],
         out_shape=jax.ShapeDtypeStruct(fields.shape, jnp.float32),
-        input_output_aliases={5: 0},
-        scratch_shapes=[pltpu.VMEM((cosines.shape[0] * 2 * BS, left.shape[1]), jnp.bfloat16)],
-        compiler_params=CP,
-        name="fields_second",
-    )(block_order, parts, cosines, sines, left, fields, after)
+        input_output_aliases={3: 0},
+        scratch_shapes=[pltpu.VMEM((cosines.shape[0] * columns * BS, left.shape[1]), jnp.bfloat16)],
+        compiler_params=CP,
+        name="fields_more",
+    )(cosines, sines, left, fields, after)
 
 
 ROWS = 512
@@ -222,11 +223,15 @@
     for hop in range(8):
         send, g = step(1, hop, nrm, fields, g, r)
         r = lax.ppermute(send, "sa", up)
+        if hop == 0:
+            fields = more_columns(slice(1, 2), made, fields, g, scale)
+        if hop == 1:
+            fields = more_columns(slice(2, 3), made, fields, g, scale)
         if hop < 7:
             send, g = step(-1, hop, nrm, fields, g, l)
             l = lax.ppermute(send, "sa", down)
         if hop == 0:
-            fields = second_half(parts, block_order, made, g, scale)
+            fields = more_columns(slice(3, 4), made, fields, g, scale)
     tiles, nsum = pl.pallas_call(
         lambda *refs: final_kernel(entries, *refs),
         in_specs=vm(5),

time: 113 us -> 113 us (level)
  waiting for transfers between devices: 21.7 us -> 18 us
  starting transfers between devices: 54.8 us -> 57.3 us
  local copies, waits for them, and re-layouts: 2.23 us -> 3.54 us
    ppermute x8, waiting for transfers between devices: 21.6 us -> 15.4 us  [body(): r = lax.ppermute(send, 'sa', up)]
    ppermute x7, waiting for transfers between devices: 0.02 us -> 2.58 us  [body(): l = lax.ppermute(send, 'sa', down)]
    ppermute x7, starting transfers between devices: 37 us -> 39.5 us  [body(): l = lax.ppermute(send, 'sa', down)]
    unnamed x6, local copies, waits for them, and re-layouts: 2.23 us -> 3.54 us
    pallas_call x1, Pallas kernels: 3.54 us -> 2.3 us  [first_half(): pl.pallas_call(lambda *refs: first_kernel(scale, *refs), in_specs=[pl.Blo...]
    pallas_call x1 -> x3, Pallas kernels: 3.24 us -> 4.45 us  [more_columns(): pl.pallas_call(lambda *refs: more_kernel(cut, scale, *refs), in_specs=vm(...]
  transfers between devices with their start and end apart: 15 -> 15, of which waited for: 8 -> 14; matrix products, arithmetic and copies ran while one was open for 0% -> 0% of each run, Pallas kernels for 3% -> 4%
where the time goes in v6:
time: 113 us; the launch traced here: 112 us
  starting transfers between devices  57.3 us (51%)
  blocking collectives  24.5 us (22%)
  waiting for transfers between devices  18 us (16%)
  Pallas kernels  8.04 us (7%)
  local copies, waits for them, and re-layouts  3.54 us (3%)
    ppermute x7, starting transfers between devices, body(): l = lax.ppermute(send, 'sa', down)  39.5 us
    all_to_all x1, blocking collectives, body(): tiles = lax.all_to_all(tiles, 'ta', 0, 0, tiled=True)  24.5 us
    ppermute x8, starting transfers between devices, body(): r = lax.ppermute(send, 'sa', up)  17.8 us
    ppermute x8, waiting for transfers between devices, body(): r = lax.ppermute(send, 'sa', up)  15.4 us
    pallas_call x3, Pallas kernels, more_columns(): pl.pallas_call(lambda *refs: more_kernel(cut, scale, *refs), in_specs=vm(...  4.45 us
    unnamed x6, local copies, waits for them, and re-layouts  3.54 us
    ppermute x7, waiting for transfers between devices, body(): l = lax.ppermute(send, 'sa', down)  2.58 us
    pallas_call x1, Pallas kernels, first_half(): pl.pallas_call(lambda *refs: first_kernel(scale, *refs), in_specs=[pl.Blo...  2.3 us
  transfers between devices with their start and end apart: 15, of which 14 were waited for; matrix products, arithmetic and copies ran while one was open for 0% of the time, Pallas kernels for 4%

profile of v6, /device:TPU:1, one launch (start us, length us, event | category | flops | bytes accessed | tf_op | source)
XLA Modules:
  0.0 112.2 jit_solution(17581267127615305001)
XLA Ops:
  0.6 1.4 %copy.23 = bf16[1,256,2,3,1,384]{5,1,3,2,4,0:T(8,128)(2,1)S(1)} copy(bf16[1,256,2,3,1,384]{5,2,4,3,1,0:T(2,128)(2,1)} %param.3) | data formatting | bytes 2359296 | tf_op args[0]
  2.1 0.0 copy-start
  2.1 0.7 copy-done
  2.7 0.0 copy-start.1
  2.7 0.7 copy-done.1
  3.4 2.3 %fields_first.1 = (f32[16,8,64,128]{3,2,1,0:T(8,128)S(1)}, f32[8,128]{1,0:T(8,128)S(1)}, bf16[512,2304]{1,0:T(8,128)(2,1)S(1)}, f32[8,384]{1,0:T(8,128)S(1)}, f32[8,384]{1,0:T(8,128)S(1)}) custom-call(s32[4]{0:T(128)S(1)} %copy-done.1, s32[3,8]{1,0:T(4,128)S(1)} %bitcast.8, bf16[6,256,384]{2,1,0:T(8,128)(2,1)S(1)} %bitcast.7), custom_call_target="tpu_custom_call" | custom-call | tf_op jit(solution)/shard_map/fields_first/pallas_call | solution.py:110
  5.7 4.4 %collective-permute-start = (f32[520,128]{1,0:T(8,128)S(1)}, f32[520,128]{1,0:T(8,128)S(1)}, u32[]{:S(2)}, u32[]{:S(2)}) collective-permute-start(f32[520,128]{1,0:T(8,128)S(1)} %get-tuple-element.46), channel_id=1, source_target_pairs={{0,1},{1,2},{2,3},{3,4},{4,5},{5,6},{6,7},{7,8},{8,9},{9,10},{10,1... | collective-permute-start | bytes 798728 | tf_op jit(solution)/shard_map/ppermute | solution.py:225
  10.1 1.5 %fields_more.3.refs_1_.refs_3_ = f32[16,8,64,128]{3,2,1,0:T(8,128)S(1)} custom-call(f32[8,384]{1,0:T(8,128)S(1)} %get-tuple-element.40.refs_0_, f32[8,384]{1,0:T(8,128)S(1)} %get-tuple-element.41.refs_1_, bf16[512,2304]{1,0:T(8,128)(2,1)S(1)} %get-tuple-element.42.refs_2_, ...), custom_call_target="tpu_custom_call", output_to_operand_aliasing={{}: (3, {})} | custom-call | tf_op jit(solution)/shard_map/fields_more/pallas_call | solution.py:130
  11.7 9.5 %collective-permute-start.1 = (f32[520,128]{1,0:T(8,128)S(1)}, f32[520,128]{1,0:T(8,128)S(1)}, u32[]{:S(2)}, u32[]{:S(2)}) collective-permute-start(f32[520,128]{1,0:T(8,128)S(1)} %get-tuple-element.48), channel_id=1, source_target_pairs={{0,15},{1,0},{2,1},{3,2},{4,3},{5,4},{6,5},{7,6},{8,7},{9,8},{10,9... | collective-permute-start | bytes 798728 | tf_op jit(solution)/shard_map/ppermute | solution.py:232
  21.2 1.5 %fields_more.4.refs_1_.refs_3_ = f32[16,8,64,128]{3,2,1,0:T(8,128)S(1)} custom-call(f32[8,384]{1,0:T(8,128)S(1)} %get-tuple-element.40.refs_0_, f32[8,384]{1,0:T(8,128)S(1)} %get-tuple-element.41.refs_1_, bf16[512,2304]{1,0:T(8,128)(2,1)S(1)} %get-tuple-element.42.refs_2_, ...), custom_call_target="tpu_custom_call", output_to_operand_aliasing={{}: (3, {})} | custom-call | tf_op jit(solution)/shard_map/fields_more/pallas_call | solution.py:130
  22.7 1.2 %collective-permute-done.refs_3_ = f32[520,128]{1,0:T(8,128)S(1)} collective-permute-done((f32[520,128]{1,0:T(8,128)S(1)}, f32[520,128]{1,0:T(8,128)S(1)}, u32[]{:S(2)}, u32[]{:S(2)}) %collective-permute-start) | collective-permute-done | bytes 266272 | tf_op jit(solution)/shard_map/ppermute | solution.py:225
  23.8 1.9 %collective-permute-start.2 = (f32[520,128]{1,0:T(8,128)S(1)}, f32[520,128]{1,0:T(8,128)S(1)}, u32[]{:S(2)}, u32[]{:S(2)}) collective-permute-start(f32[520,128]{1,0:T(8,128)S(1)} %get-tuple-element.50), channel_id=1, source_target_pairs={{0,1},{1,2},{2,3},{3,4},{4,5},{5,6},{6,7},{7,8},{8,9},{9,10},{10,1... | collective-permute-start | bytes 798728 | tf_op jit(solution)/shard_map/ppermute | solution.py:225
  25.8 1.5 %fields_more.5.refs_1_ = f32[16,8,64,128]{3,2,1,0:T(8,128)S(1)} custom-call(f32[8,384]{1,0:T(8,128)S(1)} %get-tuple-element.40.refs_0_, f32[8,384]{1,0:T(8,128)S(1)} %get-tuple-element.41.refs_1_, bf16[512,2304]{1,0:T(8,128)(2,1)S(1)} %get-tuple-element.42.refs_2_, ...), custom_call_target="tpu_custom_call", output_to_operand_aliasing={{}: (3, {})} | custom-call | tf_op jit(solution)/shard_map/fields_more/pallas_call | solution.py:130
  27.3 0.0 collective-permute-done.1.refs_3_
  27.3 4.6 %collective-permute-start.3 = (f32[520,128]{1,0:T(8,128)S(1)}, f32[520,128]{1,0:T(8,128)S(1)}, u32[]{:S(2)}, u32[]{:S(2)}) collective-permute-start(f32[520,128]{1,0:T(8,128)S(1)} %get-tuple-element.52), channel_id=1, source_target_pairs={{0,15},{1,0},{2,1},{3,2},{4,3},{5,4},{6,5},{7,6},{8,7},{9,8},{10,9... | collective-permute-start | bytes 798728 | tf_op jit(solution)/shard_map/ppermute | solution.py:232
  31.9 1.7 %collective-permute-done.2.refs_3_ = f32[520,128]{1,0:T(8,128)S(1)} collective-permute-done((f32[520,128]{1,0:T(8,128)S(1)}, f32[520,128]{1,0:T(8,128)S(1)}, u32[]{:S(2)}, u32[]{:S(2)}) %collective-permute-start.2) | collective-permute-done | bytes 266272 | tf_op jit(solution)/shard_map/ppermute | solution.py:225
  33.6 1.9 %collective-permute-start.4 = (f32[520,128]{1,0:T(8,128)S(1)}, f32[520,128]{1,0:T(8,128)S(1)}, u32[]{:S(2)}, u32[]{:S(2)}) collective-permute-start(f32[520,128]{1,0:T(8,128)S(1)} %get-tuple-element.54), channel_id=1, source_target_pairs={{0,1},{1,2},{2,3},{3,4},{4,5},{5,6},{6,7},{7,8},{8,9},{9,10},{10,1... | collective-permute-start | bytes 798728 | tf_op jit(solution)/shard_map/ppermute | solution.py:225
  35.6 0.5 collective-permute-done.3.refs_3_
  36.1 5.3 %collective-permute-start.5 = (f32[520,128]{1,0:T(8,128)S(1)}, f32[520,128]{1,0:T(8,128)S(1)}, u32[]{:S(2)}, u32[]{:S(2)}) collective-permute-start(f32[520,128]{1,0:T(8,128)S(1)} %get-tuple-element.56), channel_id=1, source_target_pairs={{0,15},{1,0},{2,1},{3,2},{4,3},{5,4},{6,5},{7,6},{8,7},{9,8},{10,9... | collective-permute-start | bytes 798728 | tf_op jit(solution)/shard_map/ppermute | solution.py:232
  41.4 1.1 collective-permute-done.4.refs_3_
  42.5 1.9 %collective-permute-start.6 = (f32[520,128]{1,0:T(8,128)S(1)}, f32[520,128]{1,0:T(8,128)S(1)}, u32[]{:S(2)}, u32[]{:S(2)}) collective-permute-start(f32[520,128]{1,0:T(8,128)S(1)} %get-tuple-element.58), channel_id=1, source_target_pairs={{0,1},{1,2},{2,3},{3,4},{4,5},{5,6},{6,7},{7,8},{8,9},{9,10},{10,1... | collective-permute-start | bytes 798728 | tf_op jit(solution)/shard_map/ppermute | solution.py:225
  44.4 0.3 collective-permute-done.5.refs_3_
  44.8 5.0 %collective-permute-start.7 = (f32[520,128]{1,0:T(8,128)S(1)}, f32[520,128]{1,0:T(8,128)S(1)}, u32[]{:S(2)}, u32[]{:S(2)}) collective-permute-start(f32[520,128]{1,0:T(8,128)S(1)} %get-tuple-element.60), channel_id=1, source_target_pairs={{0,15},{1,0},{2,1},{3,2},{4,3},{5,4},{6,5},{7,6},{8,7},{9,8},{10,9... | collective-permute-start | bytes 798728 | tf_op jit(solution)/shard_map/ppermute | solution.py:232
  49.8 1.1 collective-permute-done.6.refs_3_
  50.9 1.9 %collective-permute-start.8 = (f32[520,128]{1,0:T(8,128)S(1)}, f32[520,128]{1,0:T(8,128)S(1)}, u32[]{:S(2)}, u32[]{:S(2)}) collective-permute-start(f32[520,128]{1,0:T(8,128)S(1)} %get-tuple-element.62), channel_id=1, source_target_pairs={{0,1},{1,2},{2,3},{3,4},{4,5},{5,6},{6,7},{7,8},{8,9},{9,10},{10,1... | collective-permute-start | bytes 798728 | tf_op jit(solution)/shard_map/ppermute | solution.py:225
  52.8 0.3 collective-permute-done.7.refs_3_
  53.2 5.0 %collective-permute-start.9 = (f32[520,128]{1,0:T(8,128)S(1)}, f32[520,128]{1,0:T(8,128)S(1)}, u32[]{:S(2)}, u32[]{:S(2)}) collective-permute-start(f32[520,128]{1,0:T(8,128)S(1)} %get-tuple-element.64), channel_id=1, source_target_pairs={{0,15},{1,0},{2,1},{3,2},{4,3},{5,4},{6,5},{7,6},{8,7},{9,8},{10,9... | collective-permute-start | bytes 798728 | tf_op jit(solution)/shard_map/ppermute | solution.py:232
  58.2 1.1 collective-permute-done.8.refs_3_
  59.3 1.9 %collective-permute-start.10 = (f32[520,128]{1,0:T(8,128)S(1)}, f32[520,128]{1,0:T(8,128)S(1)}, u32[]{:S(2)}, u32[]{:S(2)}) collective-permute-start(f32[520,128]{1,0:T(8,128)S(1)} %get-tuple-element.66), channel_id=1, source_target_pairs={{0,1},{1,2},{2,3},{3,4},{4,5},{5,6},{6,7},{7,8},{8,9},{9,10},{10,1... | collective-permute-start | bytes 798728 | tf_op jit(solution)/shard_map/ppermute | solution.py:225
  61.3 0.3 collective-permute-done.9.refs_3_
  61.6 5.0 %collective-permute-start.11 = (f32[520,128]{1,0:T(8,128)S(1)}, f32[520,128]{1,0:T(8,128)S(1)}, u32[]{:S(2)}, u32[]{:S(2)}) collective-permute-start(f32[520,128]{1,0:T(8,128)S(1)} %get-tuple-element.68), channel_id=1, source_target_pairs={{0,15},{1,0},{2,1},{3,2},{4,3},{5,4},{6,5},{7,6},{8,7},{9,8},{10,9... | collective-permute-start | bytes 798728 | tf_op jit(solution)/shard_map/ppermute | solution.py:232
  66.6 1.1 collective-permute-done.10.refs_3_
  67.7 1.9 %collective-permute-start.12 = (f32[520,128]{1,0:T(8,128)S(1)}, f32[520,128]{1,0:T(8,128)S(1)}, u32[]{:S(2)}, u32[]{:S(2)}) collective-permute-start(f32[520,128]{1,0:T(8,128)S(1)} %get-tuple-element.70), channel_id=1, source_target_pairs={{0,1},{1,2},{2,3},{3,4},{4,5},{5,6},{6,7},{7,8},{8,9},{9,10},{10,1... | collective-permute-start | bytes 798728 | tf_op jit(solution)/shard_map/ppermute | solution.py:225
  69.7 0.3 collective-permute-done.11.refs_3_
  70.0 5.0 %collective-permute-start.14 = (f32[520,128]{1,0:T(8,128)S(1)}, f32[520,128]{1,0:T(8,128)S(1)}, u32[]{:S(2)}, u32[]{:S(2)}) collective-permute-start(f32[520,128]{1,0:T(8,128)S(1)} %get-tuple-element.73), channel_id=1, source_target_pairs={{0,15},{1,0},{2,1},{3,2},{4,3},{5,4},{6,5},{7,6},{8,7},{9,8},{10,9... | collective-permute-start | bytes 798728 | tf_op jit(solution)/shard_map/ppermute | solution.py:232
  75.0 1.3 %collective-permute-done.12.refs_3_ = f32[520,128]{1,0:T(8,128)S(1)} collective-permute-done((f32[520,128]{1,0:T(8,128)S(1)}, f32[520,128]{1,0:T(8,128)S(1)}, u32[]{:S(2)}, u32[]{:S(2)}) %collective-permute-start.12) | collective-permute-done | bytes 266272 | tf_op jit(solution)/shard_map/ppermute | solution.py:225
  76.4 1.9 %collective-permute-start.13 = (f32[520,128]{1,0:T(8,128)S(1)}, f32[520,128]{1,0:T(8,128)S(1)}, u32[]{:S(2)}, u32[]{:S(2)}) collective-permute-start(f32[520,128]{1,0:T(8,128)S(1)} %get-tuple-element.72), channel_id=1, source_target_pairs={{0,1},{1,2},{2,3},{3,4},{4,5},{5,6},{6,7},{7,8},{8,9},{9,10},{10,1... | collective-permute-start | bytes 798728 | tf_op jit(solution)/shard_map/ppermute | solution.py:225
  78.3 0.8 collective-permute-done.14.refs_4_
  79.2 7.0 %collective-permute-done.13.refs_3_ = f32[520,128]{1,0:T(8,128)S(1)} collective-permute-done((f32[520,128]{1,0:T(8,128)S(1)}, f32[520,128]{1,0:T(8,128)S(1)}, u32[]{:S(2)}, u32[]{:S(2)}) %collective-permute-start.13) | collective-permute-done | bytes 266272 | tf_op jit(solution)/shard_map/ppermute | solution.py:225
  86.2 0.8 final.1
  87.0 24.5 %all_to_all.5 = f32[32,16,128]{2,1,0:T(8,128)S(1)} all-to-all(f32[32,16,128]{2,1,0:T(8,128)S(1)} %get-tuple-element.74), channel_id=1, replica_groups=mesh['ta'=32,'sa'=16] {'ta'}, dimensions={0} | all-to-all | bytes 524288 | tf_op jit(solution)/shard_map/all_to_all | solution.py:244
  111.4 0.8 copy.24
  (16 shorter events, 0.5 us)
Async XLA Ops:
  2.1 0.7 copy-start
  2.7 0.7 copy-start.1
  5.7 18.1 %collective-permute-start = (f32[520,128]{1,0:T(8,128)S(1)}, f32[520,128]{1,0:T(8,128)S(1)}, u32[]{:S(2)}, u32[]{:S(2)}) collective-permute-start(f32[520,128]{1,0:T(8,128)S(1)} %get-tuple-element.46), channel_id=1, source_target_pairs={{0,1},{1,2},{2,3},{3,4},{4,5},{5,6},{6,7},{7,8},{8,9},{9,10},{10,1... | collective-permute-start | bytes 798728 | tf_op jit(solution)/shard_map/ppermute | solution.py:225
  11.7 15.6 %collective-permute-start.1 = (f32[520,128]{1,0:T(8,128)S(1)}, f32[520,128]{1,0:T(8,128)S(1)}, u32[]{:S(2)}, u32[]{:S(2)}) collective-permute-start(f32[520,128]{1,0:T(8,128)S(1)} %get-tuple-element.48), channel_id=1, source_target_pairs={{0,15},{1,0},{2,1},{3,2},{4,3},{5,4},{6,5},{7,6},{8,7},{9,8},{10,9... | collective-permute-start | bytes 798728 | tf_op jit(solution)/shard_map/ppermute | solution.py:232
  23.8 9.8 %collective-permute-start.2 = (f32[520,128]{1,0:T(8,128)S(1)}, f32[520,128]{1,0:T(8,128)S(1)}, u32[]{:S(2)}, u32[]{:S(2)}) collective-permute-start(f32[520,128]{1,0:T(8,128)S(1)} %get-tuple-element.50), channel_id=1, source_target_pairs={{0,1},{1,2},{2,3},{3,4},{4,5},{5,6},{6,7},{7,8},{8,9},{9,10},{10,1... | collective-permute-start | bytes 798728 | tf_op jit(solution)/shard_map/ppermute | solution.py:225
  27.3 8.7 %collective-permute-start.3 = (f32[520,128]{1,0:T(8,128)S(1)}, f32[520,128]{1,0:T(8,128)S(1)}, u32[]{:S(2)}, u32[]{:S(2)}) collective-permute-start(f32[520,128]{1,0:T(8,128)S(1)} %get-tuple-element.52), channel_id=1, source_target_pairs={{0,15},{1,0},{2,1},{3,2},{4,3},{5,4},{6,5},{7,6},{8,7},{9,8},{10,9... | collective-permute-start | bytes 798728 | tf_op jit(solution)/shard_map/ppermute | solution.py:232
  33.6 8.8 %collective-permute-start.4 = (f32[520,128]{1,0:T(8,128)S(1)}, f32[520,128]{1,0:T(8,128)S(1)}, u32[]{:S(2)}, u32[]{:S(2)}) collective-permute-start(f32[520,128]{1,0:T(8,128)S(1)} %get-tuple-element.54), channel_id=1, source_target_pairs={{0,1},{1,2},{2,3},{3,4},{4,5},{5,6},{6,7},{7,8},{8,9},{9,10},{10,1... | collective-permute-start | bytes 798728 | tf_op jit(solution)/shard_map/ppermute | solution.py:225
  36.1 8.7 %collective-permute-start.5 = (f32[520,128]{1,0:T(8,128)S(1)}, f32[520,128]{1,0:T(8,128)S(1)}, u32[]{:S(2)}, u32[]{:S(2)}) collective-permute-start(f32[520,128]{1,0:T(8,128)S(1)} %get-tuple-element.56), channel_id=1, source_target_pairs={{0,15},{1,0},{2,1},{3,2},{4,3},{5,4},{6,5},{7,6},{8,7},{9,8},{10,9... | collective-permute-start | bytes 798728 | tf_op jit(solution)/shard_map/ppermute | solution.py:232
  42.5 8.4 %collective-permute-start.6 = (f32[520,128]{1,0:T(8,128)S(1)}, f32[520,128]{1,0:T(8,128)S(1)}, u32[]{:S(2)}, u32[]{:S(2)}) collective-permute-start(f32[520,128]{1,0:T(8,128)S(1)} %get-tuple-element.58), channel_id=1, source_target_pairs={{0,1},{1,2},{2,3},{3,4},{4,5},{5,6},{6,7},{7,8},{8,9},{9,10},{10,1... | collective-permute-start | bytes 798728 | tf_op jit(solution)/shard_map/ppermute | solution.py:225
  44.8 8.4 %collective-permute-start.7 = (f32[520,128]{1,0:T(8,128)S(1)}, f32[520,128]{1,0:T(8,128)S(1)}, u32[]{:S(2)}, u32[]{:S(2)}) collective-permute-start(f32[520,128]{1,0:T(8,128)S(1)} %get-tuple-element.60), channel_id=1, source_target_pairs={{0,15},{1,0},{2,1},{3,2},{4,3},{5,4},{6,5},{7,6},{8,7},{9,8},{10,9... | collective-permute-start | bytes 798728 | tf_op jit(solution)/shard_map/ppermute | solution.py:232
  50.9 8.4 %collective-permute-start.8 = (f32[520,128]{1,0:T(8,128)S(1)}, f32[520,128]{1,0:T(8,128)S(1)}, u32[]{:S(2)}, u32[]{:S(2)}) collective-permute-start(f32[520,128]{1,0:T(8,128)S(1)} %get-tuple-element.62), channel_id=1, source_target_pairs={{0,1},{1,2},{2,3},{3,4},{4,5},{5,6},{6,7},{7,8},{8,9},{9,10},{10,1... | collective-permute-start | bytes 798728 | tf_op jit(solution)/shard_map/ppermute | solution.py:225
  53.2 8.4 %collective-permute-start.9 = (f32[520,128]{1,0:T(8,128)S(1)}, f32[520,128]{1,0:T(8,128)S(1)}, u32[]{:S(2)}, u32[]{:S(2)}) collective-permute-start(f32[520,128]{1,0:T(8,128)S(1)} %get-tuple-element.64), channel_id=1, source_target_pairs={{0,15},{1,0},{2,1},{3,2},{4,3},{5,4},{6,5},{7,6},{8,7},{9,8},{10,9... | collective-permute-start | bytes 798728 | tf_op jit(solution)/shard_map/ppermute | solution.py:232
  59.3 8.4 %collective-permute-start.10 = (f32[520,128]{1,0:T(8,128)S(1)}, f32[520,128]{1,0:T(8,128)S(1)}, u32[]{:S(2)}, u32[]{:S(2)}) collective-permute-start(f32[520,128]{1,0:T(8,128)S(1)} %get-tuple-element.66), channel_id=1, source_target_pairs={{0,1},{1,2},{2,3},{3,4},{4,5},{5,6},{6,7},{7,8},{8,9},{9,10},{10,1... | collective-permute-start | bytes 798728 | tf_op jit(solution)/shard_map/ppermute | solution.py:225
  61.6 8.4 %collective-permute-start.11 = (f32[520,128]{1,0:T(8,128)S(1)}, f32[520,128]{1,0:T(8,128)S(1)}, u32[]{:S(2)}, u32[]{:S(2)}) collective-permute-start(f32[520,128]{1,0:T(8,128)S(1)} %get-tuple-element.68), channel_id=1, source_target_pairs={{0,15},{1,0},{2,1},{3,2},{4,3},{5,4},{6,5},{7,6},{8,7},{9,8},{10,9... | collective-permute-start | bytes 798728 | tf_op jit(solution)/shard_map/ppermute | solution.py:232
  67.7 8.7 %collective-permute-start.12 = (f32[520,128]{1,0:T(8,128)S(1)}, f32[520,128]{1,0:T(8,128)S(1)}, u32[]{:S(2)}, u32[]{:S(2)}) collective-permute-start(f32[520,128]{1,0:T(8,128)S(1)} %get-tuple-element.70), channel_id=1, source_target_pairs={{0,1},{1,2},{2,3},{3,4},{4,5},{5,6},{6,7},{7,8},{8,9},{9,10},{10,1... | collective-permute-start | bytes 798728 | tf_op jit(solution)/shard_map/ppermute | solution.py:225
  70.0 9.2 %collective-permute-start.14 = (f32[520,128]{1,0:T(8,128)S(1)}, f32[520,128]{1,0:T(8,128)S(1)}, u32[]{:S(2)}, u32[]{:S(2)}) collective-permute-start(f32[520,128]{1,0:T(8,128)S(1)} %get-tuple-element.73), channel_id=1, source_target_pairs={{0,15},{1,0},{2,1},{3,2},{4,3},{5,4},{6,5},{7,6},{8,7},{9,8},{10,9... | collective-permute-start | bytes 798728 | tf_op jit(solution)/shard_map/ppermute | solution.py:232
  76.4 9.7 %collective-permute-start.13 = (f32[520,128]{1,0:T(8,128)S(1)}, f32[520,128]{1,0:T(8,128)S(1)}, u32[]{:S(2)}, u32[]{:S(2)}) collective-permute-start(f32[520,128]{1,0:T(8,128)S(1)} %get-tuple-element.72), channel_id=1, source_target_pairs={{0,1},{1,2},{2,3},{3,4},{4,5},{5,6},{6,7},{7,8},{8,9},{9,10},{10,1... | collective-permute-start | bytes 798728 | tf_op jit(solution)/shard_map/ppermute | solution.py:225
